TPU v7x, 32 devices: a whole 2x2x4 slice. The times are simulated.
32 devices in a mesh: row: 8 (over y, x, core), col: 4 (over z).
Axes of the slice: x: 2, y: 2, z: 4, core: 2. Of those that a mesh axis runs over, the one named last changes fastest.
Arguments:
- embedding: bfloat16 [512, 256, 256], P('row', 'col'), may hold values from -6 to 6
- counts: int32 [4, 8], P('col'), may hold values from 1 to 48, 128 in all within a row
- points: int32 [8, 4, 2, 48], P('row', 'col'), may hold values from 0 to 1023
- pe_gauss: float32 [2, 128], replicated, may hold values from -6 to 6
- point_embed: float32 [256], replicated, may hold values from -6 to 6
- mask_token: float32 [256], replicated, may hold values from -6 to 6
- sa_qkv: bfloat16 [256, 768], replicated, may hold values from -0.375 to 0.375
- sa_out: bfloat16 [256, 256], replicated, may hold values from -0.375 to 0.375
- t2i_qkv: bfloat16 [256, 384], replicated, may hold values from -0.375 to 0.375
- t2i_out: bfloat16 [128, 256], replicated, may hold values from -0.5 to 0.5
- mlp_up: bfloat16 [256, 2048], replicated, may hold values from -0.375 to 0.375
- mlp_down: bfloat16 [2048, 256], replicated, may hold values from -0.125 to 0.125
- i2t_qkv: bfloat16 [256, 384], replicated, may hold values from -0.375 to 0.375
- i2t_out: bfloat16 [128, 256], replicated, may hold values from -0.5 to 0.5
- hyper_w: bfloat16 [2, 256, 256], replicated, may hold values from -0.375 to 0.375
- ln_gains: float32 [4, 256], replicated, may hold values from 0.1 to 1.9
Outputs:
- mask_logits: bfloat16 [8, 4, 48, 4096], P('row', 'col')
- seam_blend: float32 [512, 256], P('row', 'col')
Inputs may be any that keep to these rules, and one draw needn't show every extreme that they name: For each column index the counts of its 8 tiles sum to 128, and the largest of them is 48. `points`: slots at or past a tile's count hold coordinates that no output reads.
All inputs are finite; a program needn't handle non-finite values.
Results may differ from a plain program's by a relative error of at most 0.012.
Values may be sent and summed in bfloat16 or wider, within the bound.
No kernel may reach another device: no remote copies, remote signals or barrier semaphores. Data moves between devices by JAX's collectives and lax.ppermute only.
A program may use at most 128 MiB of HBM per device.

v0:
```python
import math

import jax
import jax.numpy as jnp
from jax import lax
from jax.sharding import PartitionSpec as P

HEADS = 8
SEAM = 4
IMG = 1024


norm_eps = 1e-05
highest = lax.Precision.HIGHEST


def padded_2(cells, sides, width):
    for axis, dim in sides:
        count = lax.axis_size(axis)
        ends = count - 1
        head = lax.slice_in_dim(cells, 0, width, axis=dim)
        tail = lax.slice_in_dim(cells, cells.shape[dim] - width, cells.shape[dim], axis=dim)
        cells = jnp.concatenate(
            [
                lax.ppermute(tail, axis, [(i, (i + 1) % count) for i in range(ends)]),
                cells,
                lax.ppermute(head, axis, [((i + 1) % count, i) for i in range(ends)]),
            ],
            axis=dim,
        )
    return cells


def layer_norm(values, norm_gain):
    row_mean = jnp.mean(values, axis=-1, keepdims=True)
    centred = values - row_mean
    row_var = jnp.mean(centred * centred, axis=-1, keepdims=True)
    return centred * lax.rsqrt(row_var + norm_eps) * norm_gain


def weight_dot(values, weight):
    return jnp.dot(values, weight.astype(jnp.float32), precision=highest)


def fourier(norm_x, norm_y, pe_gauss):
    phases = (
        2.0
        * math.pi
        * (
            (2.0 * norm_x - 1.0)[:, None] * pe_gauss[0]
            + (2.0 * norm_y - 1.0)[:, None] * pe_gauss[1]
        )
    )
    return jnp.concatenate([jnp.sin(phases), jnp.cos(phases)], axis=-1)


def dense_pe(pixel_ids, grid_side, pe_gauss):
    norm_x = ((pixel_ids % grid_side).astype(jnp.float32) + 0.5) / grid_side
    norm_y = ((pixel_ids // grid_side).astype(jnp.float32) + 0.5) / grid_side
    return fourier(norm_x, norm_y, pe_gauss)


def softmax_last(scores):
    row_top = jnp.max(scores, axis=-1, keepdims=True)
    exp_scores = jnp.exp(scores - row_top)
    return exp_scores / jnp.sum(exp_scores, axis=-1, keepdims=True)


def head_select(inner_width):
    channel_head = jnp.arange(inner_width, dtype=jnp.int32) // (inner_width // HEADS)
    return jnp.arange(HEADS, dtype=jnp.int32)[:, None] == channel_head[None, :]


def token_side(
    points_xy,
    keys_pe,
    tile_flat,
    pe_gauss,
    point_embed,
    mask_token,
    sa_qkv,
    sa_out,
    t2i_qkv,
    t2i_out,
    mlp_up,
    mlp_down,
    i2t_qkv,
    hyper_w,
    ln_gains,
):
    slot_count = points_xy.shape[1]
    model_width = keys_pe.shape[1]
    inner_width = t2i_qkv.shape[1] // 3
    self_width = model_width // HEADS
    head_width = inner_width // HEADS
    coords = (points_xy.astype(jnp.float32) + 0.5) / IMG
    prompt = fourier(coords[0], coords[1], pe_gauss) + point_embed
    start_tok = jnp.stack([jnp.broadcast_to(mask_token, (slot_count, model_width)), prompt], axis=1)
    self_qkv = weight_dot(start_tok, sa_qkv).reshape(slot_count, 2, 3, HEADS, self_width)
    self_score = jnp.einsum(
        "cqhd,ckhd->chqk", self_qkv[:, :, 0], self_qkv[:, :, 1], precision=highest
    ) / math.sqrt(self_width)
    self_out = jnp.einsum(
        "chqk,ckhd->cqhd", softmax_last(self_score), self_qkv[:, :, 2], precision=highest
    )
    queries = layer_norm(
        weight_dot(self_out.reshape(slot_count, 2, model_width), sa_out), ln_gains[0]
    )
    cross_q = weight_dot(queries + start_tok, t2i_qkv[:, :inner_width]).astype(jnp.bfloat16)
    cross_k = jnp.dot(
        keys_pe, t2i_qkv[:, inner_width : 2 * inner_width], preferred_element_type=jnp.float32
    ).astype(jnp.bfloat16)
    cross_v = jnp.dot(
        tile_flat, t2i_qkv[:, 2 * inner_width :], preferred_element_type=jnp.float32
    ).astype(jnp.bfloat16)
    selector = head_select(inner_width)
    masked_q = jnp.where(
        selector[None], cross_q.reshape(slot_count * 2, 1, inner_width), jnp.zeros((), jnp.bfloat16)
    )
    masked_q = masked_q.reshape(slot_count * 2 * HEADS, inner_width)
    cross_score = lax.dot_general(
        masked_q, cross_k, (((1,), (1,)), ((), ())), preferred_element_type=jnp.float32
    ) / math.sqrt(head_width)
    cross_prob = softmax_last(cross_score).astype(jnp.bfloat16)
    head_out = jnp.dot(cross_prob, cross_v, preferred_element_type=jnp.float32).reshape(
        slot_count * 2, HEADS, inner_width
    )
    cross_out = jnp.sum(jnp.where(selector[None], head_out, 0.0), axis=1)
    queries = layer_norm(
        queries + weight_dot(cross_out.reshape(slot_count, 2, inner_width), t2i_out), ln_gains[1]
    )
    hidden = jax.nn.relu(weight_dot(queries, mlp_up))
    queries = layer_norm(queries + weight_dot(hidden, mlp_down), ln_gains[2])
    back_k = weight_dot(queries + start_tok, i2t_qkv[:, inner_width : 2 * inner_width]).astype(
        jnp.bfloat16
    )
    back_v = weight_dot(queries, i2t_qkv[:, 2 * inner_width :]).astype(jnp.bfloat16)
    kv_rows = jnp.concatenate([back_k, back_v], axis=1)
    hyper_rows = weight_dot(jax.nn.relu(weight_dot(queries[:, 0], hyper_w[0])), hyper_w[1]).astype(
        jnp.bfloat16
    )
    return (kv_rows, hyper_rows)


def image_side(tile_rows, query_rows, kv_rows, hyper_rows, out_weight, norm_gain):
    batch_rows, pix_rows, inner_width = query_rows.shape
    head_width = inner_width // HEADS
    channel_head = jnp.arange(inner_width, dtype=jnp.int32) // head_width
    same_head = (channel_head[:, None] == channel_head[None, :]).astype(jnp.float32)
    key_gap = kv_rows[:, 0].astype(jnp.float32) - kv_rows[:, 1].astype(jnp.float32)
    value_first = kv_rows[:, 2].astype(jnp.float32)
    value_second = kv_rows[:, 3].astype(jnp.float32)
    products = query_rows.astype(jnp.float32) * key_gap[:, None, :]
    score_gap = jnp.dot(
        products.reshape(batch_rows * pix_rows, inner_width), same_head, precision=highest
    )
    weight_first = jax.nn.sigmoid(score_gap / math.sqrt(head_width)).reshape(
        batch_rows, pix_rows, inner_width
    )
    mixture = value_second[:, None, :] + weight_first * (value_first - value_second)[:, None, :]
    mixture = mixture.astype(jnp.bfloat16)
    update = jnp.einsum("bpi,id->bpd", mixture, out_weight, preferred_element_type=jnp.float32)
    normed = layer_norm(tile_rows.astype(jnp.float32) + update, norm_gain)
    model_width = normed.shape[-1]
    return (
        jnp.sum(normed * hyper_rows.astype(jnp.float32)[:, None, :], axis=-1)
        / math.sqrt(model_width)
    ).astype(jnp.bfloat16)


def shards(
    embedding,
    counts,
    points,
    pe_gauss,
    point_embed,
    mask_token,
    sa_qkv,
    sa_out,
    t2i_qkv,
    t2i_out,
    mlp_up,
    mlp_down,
    i2t_qkv,
    i2t_out,
    hyper_w,
    ln_gains,
):
    grid_side = embedding.shape[0]
    model_width = embedding.shape[2]
    inner_width = t2i_qkv.shape[1] // 3
    slot_count = points.shape[3]
    pixel_count = grid_side * grid_side
    tile_flat = embedding.reshape(pixel_count, model_width)
    image_pe = dense_pe(jnp.arange(pixel_count, dtype=jnp.int32), grid_side, pe_gauss)
    keys_pe = (tile_flat.astype(jnp.float32) + image_pe).astype(jnp.bfloat16)
    kv_rows, hyper_rows = token_side(
        points[0, 0],
        keys_pe,
        tile_flat,
        pe_gauss,
        point_embed,
        mask_token,
        sa_qkv,
        sa_out,
        t2i_qkv,
        t2i_out,
        mlp_up,
        mlp_down,
        i2t_qkv,
        hyper_w,
        ln_gains,
    )
    query_weight = i2t_qkv[:, :inner_width]
    row_index = lax.axis_index("row")
    row_count = lax.axis_size("row")
    live_counts = counts[0]
    my_count = jnp.sum(
        jnp.where(jnp.arange(row_count, dtype=jnp.int32) == row_index, live_counts, 0)
    )
    keep_slot = (jnp.arange(slot_count, dtype=jnp.int32) < my_count)[:, None]
    gathered_kv, gathered_hyper = (
        lax.all_gather(kv_rows, "row", axis=0, tiled=True),
        lax.all_gather(hyper_rows, "row", axis=0, tiled=True),
    )
    block_pixels = pixel_count // row_count
    pieces = lax.all_to_all(
        tile_flat.reshape(row_count, block_pixels, model_width),
        "row",
        split_axis=0,
        concat_axis=0,
        tiled=True,
    )
    pix_block = row_index * block_pixels + jnp.arange(block_pixels, dtype=jnp.int32)
    block_keys = (
        pieces.astype(jnp.float32) + dense_pe(pix_block, grid_side, pe_gauss)[None]
    ).astype(jnp.bfloat16)
    block_query = jnp.dot(block_keys, query_weight, preferred_element_type=jnp.float32).astype(
        jnp.bfloat16
    )
    mean_count = slot_count // 3
    packed_total = mean_count * row_count
    count_ends = jnp.cumsum(live_counts)
    count_starts = count_ends - live_counts
    packed_order = jnp.arange(packed_total, dtype=jnp.int32)
    tile_of = jnp.sum((packed_order[:, None] >= count_ends[None, :]).astype(jnp.int32), axis=1)
    owner_hot = tile_of[:, None] == jnp.arange(row_count, dtype=jnp.int32)[None, :]
    slot_of = packed_order - jnp.sum(jnp.where(owner_hot, count_starts[None, :], 0), axis=1)
    source_row = tile_of * slot_count + slot_of

    def one_block(packed_ids):
        tile_ids, row_ids = packed_ids
        return image_side(
            pieces[tile_ids],
            block_query[tile_ids],
            gathered_kv[row_ids],
            gathered_hyper[row_ids],
            i2t_out,
            ln_gains[3],
        )

    logits = lax.map(
        one_block,
        (tile_of.reshape(mean_count, row_count), source_row.reshape(mean_count, row_count)),
    )
    logits = logits.reshape(packed_total, block_pixels)
    outgoing = (
        jnp.zeros((slot_count, row_count, block_pixels), jnp.bfloat16)
        .at[slot_of, tile_of]
        .set(logits)
    )
    returned = lax.all_to_all(outgoing, "row", split_axis=1, concat_axis=1, tiled=True)
    mask_logits = returned.reshape(slot_count, pixel_count)
    coverage = jnp.sum(
        jnp.where(keep_slot, jax.nn.sigmoid(mask_logits.astype(jnp.float32)), 0.0), axis=0
    ).reshape(grid_side, grid_side)
    padded = padded_2(coverage, (("col", 1),), SEAM)
    blended = jnp.zeros_like(coverage)
    for offset in range(-SEAM, SEAM + 1):
        factor = (SEAM + 1 - abs(offset)) / (SEAM + 1) ** 2
        blended = blended + factor * padded[:, SEAM + offset : SEAM + offset + grid_side]
    return (mask_logits.reshape(1, 1, slot_count, pixel_count), blended)


def solution(mesh):
    placed = (
        P("row", "col", None),
        P("col", None),
        P("row", "col", None, None),
        P(),
        P(),
        P(),
        P(),
        P(),
        P(),
        P(),
        P(),
        P(),
        P(),
        P(),
        P(),
        P(),
    )
    return jax.shard_map(
        shards,
        mesh=mesh,
        in_specs=placed,
        out_specs=(P("row", "col", None, None), P("row", "col")),
        check_vma=False,
    )
```

profile of v0, /device:TPU:0, one launch (start us, length us, event | category | flops | bytes accessed | tf_op | source)
XLA Modules:
  0.0 459.9 jit_solution(3252532264658852434)
XLA Ops:
  0.7 5.3 %all-to-all-start = ((bf16[8,512,256]{2,1,0:T(8,128)(2,1)}), bf16[8,512,256]{2,1,0:T(8,128)(2,1)S(1)}, u32[]{:S(2)}, u32[]{:S(2)}) async-start(bf16[8,512,256]{2,1,0:T(8,128)(2,1)} %bitcast.173), calls=%async_computation | async-start | bytes 4194304 | tf_op jit(solution)/shard_map/all_to_all | solution.py:227
  13.1 3.3 fusion.125
  17.0 3.5 convolution_bitcast_fusion
  25.5 3.7 fusion.61
  29.1 9.4 %fusion.23 = (f32[4096,128]{1,0:T(8,128)}, f32[4096,128]{1,0:T(8,128)}) fusion(f32[128]{0:T(128)S(1)} %copy-done.17, f32[4096]{0:T(1024)S(1)} %copy-done.11, f32[128]{0:T(128)S(1)} %copy-done.15, f32[4096]{0:T(1024)S(1)} %get-tuple-element.231), kind=kLoop, calls=%fused_computation.56 | loop fusion | flops 2097152 | bytes 4228096 | tf_op jit(solution)/shard_map/sin | solution.py:54
  38.5 9.1 %convolution_multiply_fusion.1 = f32[768,4096]{1,0:T(8,128)} fusion(f32[4096,128]{1,0:T(8,128)} %get-tuple-element.209, f32[4096,128]{1,0:T(8,128)} %get-tuple-element.208, bf16[4096,256]{1,0:T(8,128)(2,1)} %bitcast.175, pred[8,128]{1,0:T(8,128)(4,1)S(1)} %iota_compare_fusion, bf16[96,128]{1,0:T(8,128)(2,1)S(1)} %bitcast.181, bf16[256,384]{1,0:T(8,128)(2,1)} %param.26), kind=kOutput, calls=%fused_computation.46 | convolution fusion | flops 1081704448 | bytes 18965504 | tf_op jit(solution)/shard_map/dot_general | solution.py:121
  47.6 8.3 %online-softmax = f32[768,128]{1,0:T(8,128)} custom-call(f32[768,4096]{1,0:T(8,128)} %convolution_multiply_fusion.1, f32[4096,128]{1,0:T(8,128)} %fusion.61), custom_call_target="tpu_custom_call" | custom-call | tf_op online-softmax
  59.8 10.4 %all_gather.6 = bf16[384,4,128]{2,0,1:T(8,128)(2,1)S(1)} all-gather(bf16[48,4,128]{2,0,1:T(8,128)(2,1)S(1)} %pad_maximum_fusion.3), channel_id=1, replica_groups=mesh['row'=8,'col'=4] {'row'}, dimensions={0}, use_global_device_ids=true | all-gather | bytes 442368 | tf_op jit(solution)/shard_map/all_gather | solution.py:223
  74.1 9.2 %all_gather.7 = bf16[384,256]{1,0:T(8,128)(2,1)S(1)} all-gather(bf16[48,256]{1,0:T(8,128)(2,1)S(1)} %convolution_convert_fusion.1), channel_id=1, replica_groups=mesh['row'=8,'col'=4] {'row'}, dimensions={0}, use_global_device_ids=true | all-gather | bytes 221184 | tf_op jit(solution)/shard_map/all_gather | solution.py:224
  88.1 337.4 %while.12 = (s32[]{:T(128)}, bf16[16,8,512]{2,1,0:T(8,128)(2,1)}, s32[16,8]{1,0:T(8,128)S(1)}, bf16[8,512,256]{2,1,0:T(8,128)(2,1)S(1)}, s32[16,8]{1,0:T(8,128)S...) while((s32[]{:T(128)}, bf16[16,8,512]{2,1,0:T(8,128)(2,1)}, ...), condition=%wide.region_18.19_spmd, body=%wide.region_14.18_spmd.sunk | while | flops 1090031616 | bytes 76893208 | solution.py:262
  105.3 3.3 multiply_reduce_fusion.8
  117.9 2.9 copy.87
  126.4 3.3 multiply_reduce_fusion.8
  147.4 3.3 multiply_reduce_fusion.8
  168.5 3.3 multiply_reduce_fusion.8
  189.6 3.3 multiply_reduce_fusion.8
  210.7 3.3 multiply_reduce_fusion.8
  231.8 3.3 multiply_reduce_fusion.8
  252.9 3.3 multiply_reduce_fusion.8
  274.0 3.3 multiply_reduce_fusion.8
  295.0 3.3 multiply_reduce_fusion.8
  316.1 3.3 multiply_reduce_fusion.8
  337.2 3.3 multiply_reduce_fusion.8
  358.3 3.3 multiply_reduce_fusion.8
  379.4 3.3 multiply_reduce_fusion.8
  400.4 3.3 multiply_reduce_fusion.8
  421.5 3.3 multiply_reduce_fusion.8
  425.5 11.4 %scatter_fusion = bf16[48,8,512]{2,1,0:T(8,128)(2,1)S(1)} fusion(bf16[48,8,512]{2,1,0:T(8,128)(2,1)S(1)} %broadcast_in_dim.65, s32[128]{0:T(128)S(1)} %fusion.114, bf16[128,512]{1,0:T(8,128)(2,1)} %bitcast.50), kind=kCustom, calls=%fused_computation.4 | custom fusion | bytes 394240 | tf_op jit(solution)/shard_map/scatter | solution.py:270
  437.7 3.5 all-to-all-start.1
  442.5 7.0 %all-to-all-done.1 = bf16[48,8,512]{2,0,1:T(8,128)(2,1)S(1)} async-done(((bf16[48,8,512]{2,0,1:T(8,128)(2,1)}), bf16[48,8,512]{2,0,1:T(8,128)(2,1)S(1)}, u32[]{:S(2)}, u32[]{:S(2)}) %all-to-all-start.1) | async-done | bytes 393248 | tf_op jit(solution)/shard_map/all_to_all | solution.py:272
  449.8 3.5 collective-permute-start
  455.7 3.3 collective-permute-done.1
  (551 shorter events, 310.8 us)
Async XLA Ops:
  0.6 57.0 %copy-start = (bf16[256,2048]{1,0:T(8,128)(2,1)S(1)}, bf16[256,2048]{1,0:T(8,128)(2,1)}, u32[]{:S(2)}) copy-start(bf16[256,2048]{1,0:T(8,128)(2,1)} %param.28) | copy-start | bytes 3145732
  0.6 6.5 %copy-start.20 = (f32[2,128]{1,0:T(2,128)S(1)}, f32[2,128]{1,0:T(2,128)}, u32[]{:S(2)}) copy-start(f32[2,128]{1,0:T(2,128)} %param.21) | copy-start | bytes 3076
  0.7 6.5 %copy-start.21 = (s32[1,1,2,48]{3,2,1,0:T(2,128)S(1)}, s32[1,1,2,48]{3,2,1,0:T(2,128)}, u32[]{:S(2)}) copy-start(s32[1,1,2,48]{3,2,1,0:T(2,128)} %param.20) | copy-start | bytes 1156
  0.7 7.1 %copy-start.18 = (f32[256]{0:T(256)S(1)}, f32[256]{0:T(256)}, u32[]{:S(2)}) copy-start(f32[256]{0:T(256)} %param.22) | copy-start | bytes 3076
  0.7 7.1 %copy-start.19 = (f32[256]{0:T(256)S(1)}, f32[256]{0:T(256)}, u32[]{:S(2)}) copy-start(f32[256]{0:T(256)} %param.23) | copy-start | bytes 3076
  0.7 84.6 %all-to-all-start = ((bf16[8,512,256]{2,1,0:T(8,128)(2,1)}), bf16[8,512,256]{2,1,0:T(8,128)(2,1)S(1)}, u32[]{:S(2)}, u32[]{:S(2)}) async-start(bf16[8,512,256]{2,1,0:T(8,128)(2,1)} %bitcast.173), calls=%async_computation | async-start | bytes 4194304 | tf_op jit(solution)/shard_map/all_to_all | solution.py:227
  25.4 3.7 copy-start.11
  25.5 3.7 copy-start.15
  25.5 3.7 copy-start.17
  47.6 9.5 %copy-start.12 = (bf16[128,256]{1,0:T(8,128)(2,1)S(1)}, bf16[128,256]{1,0:T(8,128)(2,1)}, u32[]{:S(2)}) copy-start(bf16[128,256]{1,0:T(8,128)(2,1)} %param.27) | copy-start | bytes 196612
  58.3 12.9 %copy-start.22 = (s32[1,8]{1,0:T(1,128)S(1)}, s32[1,8]{1,0:T(1,128)}, u32[]{:S(2)}) copy-start(s32[1,8]{1,0:T(1,128)} %param.19) | copy-start | bytes 100
  58.3 13.4 %copy-start.13 = (bf16[128,256]{1,0:T(8,128)(2,1)S(1)}, bf16[128,256]{1,0:T(8,128)(2,1)}, u32[]{:S(2)}) copy-start(bf16[128,256]{1,0:T(8,128)(2,1)} %param.31) | copy-start | bytes 196612
  105.3 3.9 copy-start.4
  113.3 2.6 copy-start.3
  126.4 3.9 copy-start.4
  147.4 3.9 copy-start.4
  168.5 3.9 copy-start.4
  189.6 3.9 copy-start.4
  210.7 3.9 copy-start.4
  231.8 3.9 copy-start.4
  252.9 3.9 copy-start.4
  274.0 3.9 copy-start.4
  295.0 3.9 copy-start.4
  316.1 3.9 copy-start.4
  337.2 3.9 copy-start.4
  358.3 3.9 copy-start.4
  379.4 3.9 copy-start.4
  400.4 3.9 copy-start.4
  421.5 3.9 copy-start.4
  437.7 11.7 %all-to-all-start.1 = ((bf16[48,8,512]{2,0,1:T(8,128)(2,1)}), bf16[48,8,512]{2,0,1:T(8,128)(2,1)S(1)}, u32[]{:S(2)}, u32[]{:S(2)}) async-start(bf16[48,8,512]{2,0,1:T(8,128)(2,1)} %copy.66), calls=%async_computation.1 | async-start | bytes 786432 | tf_op jit(solution)/shard_map/all_to_all | solution.py:272
  449.8 5.9 %collective-permute-start = (f32[64,4]{1,0:T(8,128)S(1)}, f32[64,4]{1,0:T(8,128)S(1)}, u32[]{:S(2)}, u32[]{:S(2)}) collective-permute-start(f32[64,4]{1,0:T(8,128)S(1)} %get-tuple-element.210), channel_id=1, source_target_pairs={{0,1},{1,2},{2,3},{4,5},{5,6},{6,7},{8,9},{9,10},{10,11},{12,13},{... | collective-permute-start | bytes 3080 | tf_op jit(solution)/shard_map/ppermute | solution.py:25
  453.3 5.8 %collective-permute-start.1 = (f32[64,4]{1,0:T(8,128)S(1)}, f32[64,4]{1,0:T(8,128)S(1)}, u32[]{:S(2)}, u32[]{:S(2)}) collective-permute-start(f32[64,4]{1,0:T(8,128)S(1)} %get-tuple-element.211), channel_id=1, source_target_pairs={{1,0},{2,1},{3,2},{5,4},{6,5},{7,6},{9,8},{10,9},{11,10},{13,12},{... | collective-permute-start | bytes 3080 | tf_op jit(solution)/shard_map/ppermute | solution.py:27
  (55 other events, 111.5 us)
where the time goes:
time: 464 us; the launch traced here: 460 us
  local copies, waits for them, and re-layouts  201 us (43%)
  matrix products  110 us (24%)
  other arithmetic  93.5 us (20%)
  blocking collectives  19.6 us (4%)
  starting transfers between devices  13.5 us (3%)
  waiting for transfers between devices  10.3 us (2%)
  Pallas kernels  8.27 us (2%)
    gather x32, local copies, waits for them, and re-layouts, one_block(): pieces[tile_ids]  77.3 us
    reduce_sum x16, other arithmetic, image_side(): jnp.sum(normed * hyper_rows.astype(jnp.float32)[:, None, :], axis=-1)  52.4 us
    dot_general x16, matrix products, image_side(): jnp.dot(products.reshape(batch_rows * pix_rows, inner_width), same_head,...  41.8 us
    dot_general x16, matrix products, image_side(): jnp.einsum('bpi,id->bpd', mixture, out_weight, preferred_element_type=jnp...  38.3 us
    gather x16, local copies, waits for them, and re-layouts, one_block(): block_query[tile_ids]  31.6 us
    gather x16, local copies, waits for them, and re-layouts, one_block(): gathered_kv[row_ids]  30 us
    while x128, local copies, waits for them, and re-layouts  21.2 us
    scatter x2, local copies, waits for them, and re-layouts, shards(): outgoing = jnp.zeros((slot_count, row_count, block_pixels), jnp.bfloat16)...  12.3 us
  transfers between devices with their start and end apart: 4, of which 2 were waited for; matrix products, arithmetic and copies ran while one was open for 11% of the time, Pallas kernels for 2%

commit v1 on v0

v1 whole, which is shorter than its diff:
```python
import functools
import math

import jax
import jax.numpy as jnp
from jax import lax
from jax.experimental import pallas as pl
from jax.experimental.pallas import tpu as pltpu
from jax.sharding import PartitionSpec as P

HEADS = 8
SEAM = 4
IMG = 1024
ROWS_AT_ONCE = 384
CELLS_AT_ONCE = 512

norm_eps = 1e-05
bf16 = jnp.bfloat16
f32 = jnp.float32


def mm(left, right):
    return lax.dot_general(left, right, (((1,), (0,)), ((), ())), preferred_element_type=f32)


def mm_t(left, right):
    return lax.dot_general(left, right, (((1,), (1,)), ((), ())), preferred_element_type=f32)


def halves(values):
    high = values.astype(bf16)
    low = (values - high.astype(f32)).astype(bf16)
    return jnp.concatenate([high, low], axis=0)


def wide_mm(values, weight, product=mm):
    rows = values.shape[0]
    both = product(halves(values), weight)
    return both[:rows] + both[rows:]


def layer_norm(values, gain):
    centred = values - jnp.mean(values, axis=-1, keepdims=True)
    spread = jnp.mean(centred * centred, axis=-1, keepdims=True)
    return centred * lax.rsqrt(spread + norm_eps) * gain


def sin_turns(turns):
    part = turns - jnp.floor(turns + 0.5)
    size = 0.25 - jnp.abs(jnp.abs(part) - 0.25)
    angle = (2.0 * math.pi) * jnp.where(part < 0.0, -size, size)
    square = angle * angle
    total = jnp.full_like(angle, -1.0 / math.factorial(11))
    for order in (9, 7, 5, 3, 1):
        sign = 1.0 if order % 4 == 1 else -1.0
        total = total * square + sign / math.factorial(order)
    return total * angle


def by_head(rows, inner_width):
    head_width = inner_width // HEADS
    lane = lax.broadcasted_iota(jnp.int32, rows.shape, 1)
    return jnp.concatenate(
        [
            jnp.where((lane >= h * head_width) & (lane < (h + 1) * head_width), rows, 0.0)
            for h in range(HEADS)
        ],
        axis=0,
    )


def group_ones(width, group):
    row = lax.broadcasted_iota(jnp.int32, (width, width), 0)
    column = lax.broadcasted_iota(jnp.int32, (width, width), 1)
    first = row - lax.rem(row, group)
    return jnp.where((column >= first) & (column < first + group), 1.0, 0.0).astype(bf16)


def decode_kernel(
    counts_ref,
    points_ref,
    gauss_ref,
    point_embed_ref,
    mask_token_ref,
    sa_qkv_ref,
    sa_out_ref,
    t2i_qkv_ref,
    t2i_out_ref,
    mlp_up_ref,
    mlp_down_ref,
    i2t_qkv_ref,
    i2t_out_ref,
    hyper_ref,
    gains_ref,
    cells_ref,
    logits_ref,
    coverage_ref,
    keys_ref,
    table_ref,
    pooled_ref,
):
    pixels, width = cells_ref.shape
    side = math.isqrt(pixels)
    slots = points_ref.shape[1]
    inner = t2i_qkv_ref.shape[1] // 3
    half = width // 2
    live = counts_ref[0, lax.axis_index("row")]

    gauss = gauss_ref[...]
    steps = lax.broadcasted_iota(jnp.int32, (side, half), 0).astype(f32)
    steps = (2.0 * (steps + 0.5)) / side - 1.0
    spots = jnp.clip(points_ref[...], 0, IMG - 1).astype(f32)
    spots = 2.0 * ((spots + 0.5) / IMG) - 1.0
    same = lax.broadcasted_iota(jnp.int32, (slots, slots), 0) == lax.broadcasted_iota(
        jnp.int32, (slots, slots), 1
    )
    spot_x = jnp.sum(jnp.where(same, spots[0:1], 0.0), axis=1, keepdims=True)
    spot_y = jnp.sum(jnp.where(same, spots[1:2], 0.0), axis=1, keepdims=True)
    turns = jnp.concatenate(
        [steps * gauss[0:1], steps * gauss[1:2], spot_x * gauss[0:1] + spot_y * gauss[1:2]], axis=0
    )
    sines = sin_turns(turns)
    cosines = sin_turns(turns + 0.25)
    prompt = jnp.concatenate([sines[2 * side :], cosines[2 * side :]], axis=1)
    table_ref[0] = sines[: 2 * side]
    table_ref[1] = cosines[: 2 * side]

    sin_x, cos_x = sines[:side], cosines[:side]

    def one_line(line, carry):
        sin_y = table_ref[0, pl.ds(side + line, 1), :]
        cos_y = table_ref[1, pl.ds(side + line, 1), :]
        place = pl.ds(pl.multiple_of(line * side, side), side)
        encoding = jnp.concatenate(
            [sin_x * cos_y + cos_x * sin_y, cos_x * cos_y - sin_x * sin_y], axis=1
        )
        keys_ref[place, :] = (cells_ref[place, :].astype(f32) + encoding).astype(bf16)
        return carry

    lax.fori_loop(0, side, one_line, 0, unroll=4)

    start = jnp.concatenate(
        [
            jnp.broadcast_to(mask_token_ref[...], (slots, width)),
            prompt + point_embed_ref[...],
        ],
        axis=0,
    )
    qkv = wide_mm(start, sa_qkv_ref[...])
    query, key, value = qkv[:, :width], qkv[:, width : 2 * width], qkv[:, 2 * width :]
    key_gap = key[:slots] - key[slots:]
    value_gap = value[:slots] - value[slots:]
    scores = wide_mm(
        query * jnp.concatenate([key_gap, key_gap], axis=0), group_ones(width, width // HEADS)
    )
    first = 0.5 * jnp.tanh((0.5 / math.sqrt(width // HEADS)) * scores) + 0.5
    attended = jnp.concatenate([value[slots:]] * 2, axis=0) + first * jnp.concatenate(
        [value_gap, value_gap], axis=0
    )
    queries = layer_norm(wide_mm(attended, sa_out_ref[...]), gains_ref[0:1])

    head_scale = 1.0 / math.sqrt(inner // HEADS)
    cross_q = wide_mm(queries + start, t2i_qkv_ref[:, :inner])
    cross_q = by_head(cross_q, inner).astype(bf16)
    probes = mm_t(cross_q, t2i_qkv_ref[:, inner : 2 * inner]) * (head_scale * math.log2(math.e))
    probes = probes.astype(bf16)
    probe_rows = probes.shape[0]
    for at in range(0, probe_rows, ROWS_AT_ONCE):
        raw = mm_t(probes[at : at + ROWS_AT_ONCE], keys_ref[...])
        raw = jnp.exp2(raw - jnp.max(raw, axis=1, keepdims=True))
        total = jnp.sum(raw, axis=1, keepdims=True)
        pooled_ref[at : at + ROWS_AT_ONCE, :] = mm(raw.astype(bf16), cells_ref[...]) / total
    pooled = wide_mm(pooled_ref[...], t2i_qkv_ref[:, 2 * inner :])
    tokens = start.shape[0]
    lane = lax.broadcasted_iota(jnp.int32, (tokens, inner), 1)
    head_width = inner // HEADS
    joined = jnp.zeros((tokens, inner), f32)
    for h in range(HEADS):
        own = (lane >= h * head_width) & (lane < (h + 1) * head_width)
        joined = joined + jnp.where(own, pooled[h * tokens : (h + 1) * tokens], 0.0)
    queries = layer_norm(queries + wide_mm(joined, t2i_out_ref[...]), gains_ref[1:2])
    hidden = jnp.maximum(wide_mm(queries, mlp_up_ref[...]), 0.0)
    queries = layer_norm(queries + wide_mm(hidden, mlp_down_ref[...]), gains_ref[2:3])

    back_k = wide_mm(queries + start, i2t_qkv_ref[:, inner : 2 * inner])
    back_v = wide_mm(queries, i2t_qkv_ref[:, 2 * inner :])
    gaps = by_head(back_k[:slots] - back_k[slots:], inner)
    gaps = wide_mm(gaps, i2t_qkv_ref[:, :inner], mm_t) * (0.5 * head_scale)
    gaps = gaps.astype(bf16)
    middle = 0.5 * (back_v[:slots] + back_v[slots:])
    apart = by_head(0.5 * (back_v[:slots] - back_v[slots:]), inner)
    moves = wide_mm(jnp.concatenate([apart, middle], axis=0), i2t_out_ref[...])
    moves = (moves - jnp.mean(moves, axis=1, keepdims=True)).astype(bf16)
    hyper = wide_mm(jnp.maximum(wide_mm(queries[:slots], hyper_ref[0]), 0.0), hyper_ref[1])
    hyper = hyper.astype(bf16).astype(f32) * gains_ref[3:4]
    hyper = (hyper - jnp.mean(hyper, axis=1, keepdims=True)).astype(bf16)
    spread = HEADS * slots
    apart, middle = moves[:spread], moves[spread:]
    middle_wide, hyper_wide = middle.astype(f32), hyper.astype(f32)
    middle_norm = jnp.sum(middle_wide * middle_wide, axis=1, keepdims=True)
    middle_mask = jnp.sum(middle_wide * hyper_wide, axis=1, keepdims=True)
    doubled = (2.0 * moves.astype(f32)).astype(bf16)
    on_cells = jnp.concatenate([doubled, hyper], axis=0)
    on_weights = mm_t(jnp.concatenate([apart, doubled[spread:], hyper], axis=0), apart)
    row_slot = lax.rem(lax.broadcasted_iota(jnp.int32, on_weights.shape, 0), slots)
    column_slot = lax.rem(lax.broadcasted_iota(jnp.int32, on_weights.shape, 1), slots)
    on_weights = jnp.where(row_slot == column_slot, on_weights, 0.0).astype(bf16)

    row = lax.broadcasted_iota(jnp.int32, (width, width), 0)
    column = lax.broadcasted_iota(jnp.int32, (width, width), 1)
    centring = jnp.where(row == column, 1.0 - 1.0 / width, -1.0 / width).astype(bf16)
    ones = jnp.ones((8, width), bf16)
    kept = lax.broadcasted_iota(jnp.int32, (slots, CELLS_AT_ONCE), 0) < live

    def some_cells(index, carry):
        place = pl.ds(pl.multiple_of(index * CELLS_AT_ONCE, CELLS_AT_ONCE), CELLS_AT_ONCE)
        cells = cells_ref[place, :]
        weights = jnp.tanh(mm_t(gaps, keys_ref[place, :]))
        centred = mm(cells, centring)
        squares = halves(centred * centred)
        norms = mm_t(ones, squares)
        norms = norms[:, :CELLS_AT_ONCE] + norms[:, CELLS_AT_ONCE:]
        both = mm_t(on_cells, cells) + mm(on_weights, weights.astype(bf16))
        square = both[spread : spread + slots] + middle_norm
        square = square + jnp.concatenate([norms] * (slots // 8), axis=0)
        for h in range(HEADS):
            part = slice(h * slots, (h + 1) * slots)
            square = square + weights[part] * both[part]
        dots = both[spread + slots :] + middle_mask
        logits = dots * lax.rsqrt(jnp.maximum(square, 0.0) + width * norm_eps)
        logits = jnp.where(kept, logits, 0.0).astype(bf16)
        logits_ref[:, place] = logits
        shares = jnp.where(kept, 0.5 * jnp.tanh(0.5 * logits.astype(f32)) + 0.5, 0.0)
        shares = jnp.sum(shares, axis=0, keepdims=True)
        lines = CELLS_AT_ONCE // 128
        for line in range(lines):
            coverage_ref[pl.ds(index * lines + line, 1), :] = shares[
                :, line * 128 : (line + 1) * 128
            ]
        return carry

    lax.fori_loop(0, pixels // CELLS_AT_ONCE, some_cells, 0)


def padded_2(cells, sides, width):
    for axis, dim in sides:
        count = lax.axis_size(axis)
        ends = count - 1
        head = lax.slice_in_dim(cells, 0, width, axis=dim)
        tail = lax.slice_in_dim(cells, cells.shape[dim] - width, cells.shape[dim], axis=dim)
        cells = jnp.concatenate(
            [
                lax.ppermute(tail, axis, [(i, (i + 1) % count) for i in range(ends)]),
                cells,
                lax.ppermute(head, axis, [((i + 1) % count, i) for i in range(ends)]),
            ],
            axis=dim,
        )
    return cells


def shards(
    embedding,
    counts,
    points,
    pe_gauss,
    point_embed,
    mask_token,
    sa_qkv,
    sa_out,
    t2i_qkv,
    t2i_out,
    mlp_up,
    mlp_down,
    i2t_qkv,
    i2t_out,
    hyper_w,
    ln_gains,
):
    side = embedding.shape[0]
    width = embedding.shape[2]
    inner = t2i_qkv.shape[1] // 3
    slots = points.shape[3]
    pixels = side * side
    whole = pl.BlockSpec(memory_space=pltpu.VMEM)
    logits, coverage = pl.pallas_call(
        decode_kernel,
        out_shape=(
            jax.ShapeDtypeStruct((slots, pixels), bf16),
            jax.ShapeDtypeStruct((pixels // 128, 128), f32),
        ),
        in_specs=[pl.BlockSpec(memory_space=pltpu.SMEM)] + [whole] * 15,
        out_specs=(whole, whole),
        scratch_shapes=[
            pltpu.VMEM((pixels, width), bf16),
            pltpu.VMEM((2, 2 * side, width // 2), f32),
            pltpu.VMEM((2 * slots * HEADS, width), f32),
        ],
        compiler_params=pltpu.CompilerParams(vmem_limit_bytes=58 << 20),
        name="decode",
    )(
        counts,
        points.reshape(2, slots),
        pe_gauss,
        point_embed.reshape(1, width),
        mask_token.reshape(1, width),
        sa_qkv,
        sa_out,
        t2i_qkv,
        t2i_out,
        mlp_up,
        mlp_down,
        i2t_qkv,
        i2t_out,
        hyper_w,
        ln_gains,
        embedding.reshape(pixels, width),
    )
    coverage = coverage.reshape(side, side)
    padded = padded_2(coverage, (("col", 1),), SEAM)
    blended = jnp.zeros_like(coverage)
    for offset in range(-SEAM, SEAM + 1):
        factor = (SEAM + 1 - abs(offset)) / (SEAM + 1) ** 2
        blended = blended + factor * padded[:, SEAM + offset : SEAM + offset + side]
    return (logits.reshape(1, 1, slots, pixels), blended)


def solution(mesh):
    placed = (P("row", "col", None), P("col", None), P("row", "col", None, None)) + (P(),) * 13
    return jax.shard_map(
        shards,
        mesh=mesh,
        in_specs=placed,
        out_specs=(P("row", "col", None, None), P("row", "col")),
        check_vma=False,
    )
```

time: 464 us -> 36.3 us (0.08)
  local copies, waits for them, and re-layouts: 201 us -> 0.86 us
  matrix products: 110 us -> 0 us
  other arithmetic: 93.5 us -> 0.81 us
  blocking collectives: 19.6 us -> 0 us
  Pallas kernels: 8.27 us -> 23 us
  starting transfers between devices: 13.5 us -> 6.24 us
  waiting for transfers between devices: 10.3 us -> 4.51 us
    gather x80 -> x0, local copies, waits for them, and re-layouts: 148 us -> none  [the longest x32 77.3 us: one_block(): pieces[tile_ids]]
    dot_general x47 -> x0, matrix products: 110 us -> none  [the longest x16 41.8 us: image_side(): jnp.dot(products.reshape(batch_rows * pix_rows, inner_width), same_head,...]
    reduce_sum x41 -> x0, other arithmetic: 65.1 us -> none  [the longest x16 52.4 us: image_side(): jnp.sum(normed * hyper_rows.astype(jnp.float32)[:, None, :], axis=-1)]
    pallas_call x0 -> x1, Pallas kernels: none -> 23 us  [shards(): pl.pallas_call(decode_kernel, out_shape=(jax.ShapeDtypeStruct((slots, pix...]
    while x130 -> x0, local copies, waits for them, and re-layouts: 22.4 us -> none
    all_gather x2 -> x0, blocking collectives: 19.6 us -> none  [the longest x1 10.4 us: shards(): lax.all_gather(kv_rows, 'row', axis=0, tiled=True)]
    slice x18 -> x0, local copies, waits for them, and re-layouts: 13.2 us -> none  [the longest x16 11.1 us: one_block(): ln_gains[3]]
    scatter x2 -> x0, local copies, waits for them, and re-layouts: 12.3 us -> none  [shards(): outgoing = jnp.zeros((slot_count, row_count, block_pixels), jnp.bfloat16)...]
  transfers between devices with their start and end apart: 4 -> 2, of which waited for: 2 -> 2; matrix products, arithmetic and copies ran while one was open for 11% -> 0% of each run, Pallas kernels for 2% -> 0%
where the time goes in v1:
time: 36.3 us; the launch traced here: 36.1 us
  Pallas kernels  23 us (63%)
  starting transfers between devices  6.24 us (17%)
  waiting for transfers between devices  4.51 us (12%)
  local copies, waits for them, and re-layouts  0.86 us (2%)
  other arithmetic  0.81 us (2%)
  between operations  0.65 us (2%)
    pallas_call x1, Pallas kernels, shards(): pl.pallas_call(decode_kernel, out_shape=(jax.ShapeDtypeStruct((slots, pix...  23 us
    ppermute x1, starting transfers between devices, padded_2(): lax.ppermute(tail, axis, [(i, (i + 1) % count) for i in range(ends)])  4.95 us
    ppermute x1, waiting for transfers between devices, padded_2(): lax.ppermute(head, axis, [((i + 1) % count, i) for i in range(ends)])  4.23 us
    ppermute x1, starting transfers between devices, padded_2(): lax.ppermute(head, axis, [((i + 1) % count, i) for i in range(ends)])  1.29 us
    add x1, other arithmetic, shards(): blended = blended + factor * padded[:, SEAM + offset:SEAM + offset + side]  0.81 us
    reshape x1, local copies, waits for them, and re-layouts, shards(): coverage = coverage.reshape(side, side)  0.79 us
  transfers between devices with their start and end apart: 2, of which 2 were waited for; matrix products, arithmetic and copies ran while one was open for 0% of the time, Pallas kernels for 0%

profile of v1, /device:TPU:0, one launch (start us, length us, event | category | flops | bytes accessed | tf_op | source)
XLA Modules:
  0.0 36.1 jit_solution(487889658173620698)
XLA Ops:
  0.6 23.0 %decode.1 = (bf16[48,4096]{1,0:T(8,128)(2,1)}, f32[32,128]{1,0:T(8,128)}) custom-call(s32[1,8]{1,0:T(1,128)} %counts_ref.1, s32[2,48]{1,0:T(2,128)} %bitcast.6, f32[2,128]{1,0:T(2,128)} %gauss_ref.1, f32[1,256]{1,0:T(1,128)} %bitcast.7, f32[1,256]{1,0:T(1,128)} %bitcast.8, bf16[256,768]{1,0:T(8,128)(2,1)} %sa_qkv_ref.1, bf16[256,256]{1,0:T(8,128)(2,1)} %sa_out_ref.1, ...), custom_call_target="tpu_custom_call" | custom-call | tf_op jit(solution)/shard_map/decode/pallas_call | solution.py:286
  23.7 0.8 %reshape.27 = f32[64,64]{1,0:T(8,128)S(1)} reshape(f32[32,128]{1,0:T(8,128)} %get-tuple-element.5) | data formatting | bytes 32768 | tf_op jit(solution)/shard_map/reshape | solution.py:319
  24.4 0.1 fusion.14
  24.5 5.0 %collective-permute-start = (f32[64,4]{1,0:T(8,128)S(1)}, f32[64,4]{1,0:T(8,128)S(1)}, u32[]{:S(2)}, u32[]{:S(2)}) collective-permute-start(f32[64,4]{1,0:T(8,128)S(1)} %get-tuple-element.6), channel_id=1, source_target_pairs={{0,1},{1,2},{2,3},{4,5},{5,6},{6,7},{8,9},{9,10},{10,11},{12,13},{... | collective-permute-start | bytes 3080 | tf_op jit(solution)/shard_map/ppermute | solution.py:253
  29.5 1.3 %collective-permute-start.1 = (f32[64,4]{1,0:T(8,128)S(1)}, f32[64,4]{1,0:T(8,128)S(1)}, u32[]{:S(2)}, u32[]{:S(2)}) collective-permute-start(f32[64,4]{1,0:T(8,128)S(1)} %get-tuple-element.7), channel_id=1, source_target_pairs={{1,0},{2,1},{3,2},{5,4},{6,5},{7,6},{9,8},{10,9},{11,10},{13,12},{... | collective-permute-start | bytes 3080 | tf_op jit(solution)/shard_map/ppermute | solution.py:255
  30.8 0.3 collective-permute-done
  31.1 4.2 %collective-permute-done.1 = f32[64,4]{1,0:T(8,128)S(1)} collective-permute-done((f32[64,4]{1,0:T(8,128)S(1)}, f32[64,4]{1,0:T(8,128)S(1)}, u32[]{:S(2)}, u32[]{:S(2)}) %collective-permute-start.1) | collective-permute-done | bytes 1056 | tf_op jit(solution)/shard_map/ppermute | solution.py:255
  35.3 0.8 %fusion.1 = f32[64,64]{1,0:T(8,128)} fusion(f32[64,4]{1,0:T(8,128)S(1)} %collective-permute-done.1, f32[64,64]{1,0:T(8,128)S(1)} %reshape.27, f32[64,4]{1,0:T(8,128)S(1)} %collective-permute-done), kind=kLoop, calls=%fused_computation.2 | loop fusion | flops 102400 | bytes 34816 | tf_op jit(solution)/shard_map/add | solution.py:324
Async XLA Ops:
  24.5 6.5 %collective-permute-start = (f32[64,4]{1,0:T(8,128)S(1)}, f32[64,4]{1,0:T(8,128)S(1)}, u32[]{:S(2)}, u32[]{:S(2)}) collective-permute-start(f32[64,4]{1,0:T(8,128)S(1)} %get-tuple-element.6), channel_id=1, source_target_pairs={{0,1},{1,2},{2,3},{4,5},{5,6},{6,7},{8,9},{9,10},{10,11},{12,13},{... | collective-permute-start | bytes 3080 | tf_op jit(solution)/shard_map/ppermute | solution.py:253
  29.5 5.8 %collective-permute-start.1 = (f32[64,4]{1,0:T(8,128)S(1)}, f32[64,4]{1,0:T(8,128)S(1)}, u32[]{:S(2)}, u32[]{:S(2)}) collective-permute-start(f32[64,4]{1,0:T(8,128)S(1)} %get-tuple-element.7), channel_id=1, source_target_pairs={{1,0},{2,1},{3,2},{5,4},{6,5},{7,6},{9,8},{10,9},{11,10},{13,12},{... | collective-permute-start | bytes 3080 | tf_op jit(solution)/shard_map/ppermute | solution.py:255

commit v2 on v1

v2 whole, which is shorter than its diff:
```python
import functools
import math

import jax
import jax.numpy as jnp
from jax import lax
from jax.experimental import pallas as pl
from jax.experimental.pallas import tpu as pltpu
from jax.sharding import PartitionSpec as P

HEADS = 8
SEAM = 4
IMG = 1024
SLOT_GROUP = 16
KEYS_AT_ONCE = 1024
PROBES_AT_ONCE = 256
CELLS_AT_ONCE = 512

norm_eps = 1e-05
bf16 = jnp.bfloat16
f32 = jnp.float32


def mm(left, right):
    return lax.dot_general(left, right, (((1,), (0,)), ((), ())), preferred_element_type=f32)


def mm_t(left, right):
    return lax.dot_general(left, right, (((1,), (1,)), ((), ())), preferred_element_type=f32)


def halves(values):
    high = values.astype(bf16)
    low = (values - high.astype(f32)).astype(bf16)
    return jnp.concatenate([high, low], axis=0)


def wide_mm(values, weight, product=mm):
    rows = values.shape[0]
    both = product(halves(values), weight)
    return both[:rows] + both[rows:]


def layer_norm(values, gain):
    centred = values - jnp.mean(values, axis=-1, keepdims=True)
    spread = jnp.mean(centred * centred, axis=-1, keepdims=True)
    return centred * lax.rsqrt(spread + norm_eps) * gain


def sin_turns(turns):
    part = turns - jnp.floor(turns + 0.5)
    size = 0.25 - jnp.abs(jnp.abs(part) - 0.25)
    angle = (2.0 * math.pi) * jnp.where(part < 0.0, -size, size)
    square = angle * angle
    total = jnp.full_like(angle, -1.0 / math.factorial(11))
    for order in (9, 7, 5, 3, 1):
        sign = 1.0 if order % 4 == 1 else -1.0
        total = total * square + sign / math.factorial(order)
    return total * angle


def by_head(rows, inner_width):
    head_width = inner_width // HEADS
    lane = lax.broadcasted_iota(jnp.int32, rows.shape, 1)
    return jnp.concatenate(
        [
            jnp.where((lane >= h * head_width) & (lane < (h + 1) * head_width), rows, 0.0)
            for h in range(HEADS)
        ],
        axis=0,
    )


def by_group(rows, inner_width):
    return jnp.concatenate(
        [
            by_head(rows[at : at + SLOT_GROUP], inner_width)
            for at in range(0, rows.shape[0], SLOT_GROUP)
        ],
        axis=0,
    )


def group_ones(width, group):
    row = lax.broadcasted_iota(jnp.int32, (width, width), 0)
    column = lax.broadcasted_iota(jnp.int32, (width, width), 1)
    first = row - lax.rem(row, group)
    return jnp.where((column >= first) & (column < first + group), 1.0, 0.0).astype(bf16)


def cell_weights(gaps, keys):
    return jnp.tanh(mm_t(gaps, keys)).astype(bf16)


def cell_logits(weights, cells, on_cells, on_weights, consts, live):
    count, width = cells.shape
    slots = consts.shape[0]
    block = HEADS * SLOT_GROUP
    tall = block + 2 * SLOT_GROUP
    flat = mm_t(on_cells, cells)
    wide = cells.astype(f32)
    norms = mm_t(jnp.ones((SLOT_GROUP, width), bf16), halves(wide * wide))
    total = flat[slots // SLOT_GROUP * tall :][:SLOT_GROUP]
    norms = norms[:, :count] + norms[:, count:] - total * total * (1.0 / width)
    logits, covers = [], []
    for at in range(0, slots, SLOT_GROUP):
        group = at // SLOT_GROUP
        mine = weights[group * block : (group + 1) * block]
        both = flat[group * tall : (group + 1) * tall] + mm(
            on_weights[group * tall : (group + 1) * tall], mine
        )
        square = norms + both[block : block + SLOT_GROUP] + consts[at : at + SLOT_GROUP, 0:1]
        for h in range(HEADS):
            part = slice(h * SLOT_GROUP, (h + 1) * SLOT_GROUP)
            square = square + mine[part].astype(f32) * both[part]
        dots = both[block + SLOT_GROUP :] + consts[at : at + SLOT_GROUP, 1:2]
        kept = at + lax.broadcasted_iota(jnp.int32, (SLOT_GROUP, count), 0) < live
        found = dots * lax.rsqrt(jnp.maximum(square, 0.0) + width * norm_eps)
        found = jnp.where(kept, found, 0.0).astype(bf16)
        logits.append(found)
        covers.append(jnp.where(kept, 0.5 * jnp.tanh(0.5 * found.astype(f32)) + 0.5, 0.0))
    return jnp.concatenate(logits, axis=0), jnp.sum(sum(covers), axis=0, keepdims=True)


def decode_kernel(
    counts_ref,
    points_ref,
    gauss_ref,
    point_embed_ref,
    mask_token_ref,
    sa_qkv_ref,
    sa_out_ref,
    t2i_qkv_ref,
    t2i_out_ref,
    mlp_up_ref,
    mlp_down_ref,
    i2t_qkv_ref,
    i2t_out_ref,
    hyper_ref,
    gains_ref,
    cells_ref,
    keys_ref,
    gaps_ref,
    on_cells_ref,
    on_weights_ref,
    consts_ref,
    to_left_ref,
    to_right_ref,
    seam_cells_ref,
    seam_keys_ref,
    values_ref,
    pooled_ref,
):
    pixels, width = cells_ref.shape
    side = math.isqrt(pixels)
    slots = points_ref.shape[1]
    inner = t2i_qkv_ref.shape[1] // 3
    head_width = inner // HEADS
    half = width // 2
    live = counts_ref[0, lax.axis_index("row")]

    gauss = gauss_ref[...]
    steps = lax.broadcasted_iota(jnp.int32, (side, half), 0).astype(f32)
    steps = (2.0 * (steps + 0.5)) / side - 1.0
    spots = jnp.clip(points_ref[...], 0, IMG - 1).astype(f32)
    spots = 2.0 * ((spots + 0.5) / IMG) - 1.0
    same = lax.broadcasted_iota(jnp.int32, (slots, slots), 0) == lax.broadcasted_iota(
        jnp.int32, (slots, slots), 1
    )
    spot_x = jnp.sum(jnp.where(same, spots[0:1], 0.0), axis=1, keepdims=True)
    spot_y = jnp.sum(jnp.where(same, spots[1:2], 0.0), axis=1, keepdims=True)
    turns = jnp.concatenate(
        [steps * gauss[0:1], steps * gauss[1:2], spot_x * gauss[0:1] + spot_y * gauss[1:2]], axis=0
    )
    sines = sin_turns(turns)
    cosines = sin_turns(turns + 0.25)
    prompt = jnp.concatenate([sines[2 * side :], cosines[2 * side :]], axis=1)

    start = jnp.concatenate(
        [
            jnp.broadcast_to(mask_token_ref[...], (slots, width)),
            prompt + point_embed_ref[...],
        ],
        axis=0,
    )
    qkv = wide_mm(start, sa_qkv_ref[...])
    query, key, value = qkv[:, :width], qkv[:, width : 2 * width], qkv[:, 2 * width :]
    key_gap = key[:slots] - key[slots:]
    value_gap = value[:slots] - value[slots:]
    scores = wide_mm(
        query * jnp.concatenate([key_gap, key_gap], axis=0), group_ones(width, width // HEADS)
    )
    first = 0.5 * jnp.tanh((0.5 / math.sqrt(width // HEADS)) * scores) + 0.5
    attended = jnp.concatenate([value[slots:]] * 2, axis=0) + first * jnp.concatenate(
        [value_gap, value_gap], axis=0
    )
    queries = layer_norm(wide_mm(attended, sa_out_ref[...]), gains_ref[0:1])
    head_scale = 1.0 / math.sqrt(head_width)
    cross_q = wide_mm(queries + start, t2i_qkv_ref[:, :inner])
    cross_q = by_head(cross_q, inner).astype(bf16)
    probes = mm_t(cross_q, t2i_qkv_ref[:, inner : 2 * inner]) * (head_scale * math.log2(math.e))
    probes = probes.astype(bf16)

    sin_x, cos_x = sines[:side], cosines[:side]
    left_half = lax.broadcasted_iota(jnp.int32, (2 * SEAM, width), 0) < SEAM
    for line in range(side):
        sin_y, cos_y = sines[side + line : side + line + 1], cosines[side + line : side + line + 1]
        place = slice(line * side, (line + 1) * side)
        encoding = jnp.concatenate(
            [sin_x * cos_y + cos_x * sin_y, cos_x * cos_y - sin_x * sin_y], axis=1
        )
        own = cells_ref[place, :].astype(f32)
        keys = own + encoding
        keys_ref[place, :] = keys.astype(bf16)
        seam = slice(line * 2 * SEAM, (line + 1) * 2 * SEAM)
        seam_cells_ref[seam, :] = jnp.where(left_half, own[: 2 * SEAM], own[side - 2 * SEAM :])
        seam_keys_ref[seam, :] = jnp.where(left_half, keys[: 2 * SEAM], keys[side - 2 * SEAM :])

    values_ref[...] = mm_t(
        t2i_qkv_ref[:, 2 * inner :].astype(f32).T.astype(bf16), cells_ref[...]
    ).astype(bf16)
    tokens = start.shape[0]
    for at in range(0, HEADS * tokens, PROBES_AT_ONCE):
        probe = probes[at : at + PROBES_AT_ONCE]
        rows = slice(
            at // tokens * head_width, ((at + PROBES_AT_ONCE - 1) // tokens + 1) * head_width
        )
        for cell in range(0, pixels, KEYS_AT_ONCE):
            near = slice(cell, cell + KEYS_AT_ONCE)
            raw = mm_t(keys_ref[near, :], probe)
            top = jnp.max(raw, axis=0, keepdims=True)
            if cell > 0:
                top = jnp.maximum(top, old_top)
                fade = jnp.exp2(old_top - top)
            raw = jnp.exp2(raw - top)
            total = jnp.sum(raw, axis=0, keepdims=True)
            pooled = mm(values_ref[rows, near], raw.astype(bf16))
            if cell > 0:
                total = total + fade * old_total
                pooled = pooled + fade * old_pooled
            old_top, old_total, old_pooled = top, total, pooled
        pooled_ref[rows, at : at + PROBES_AT_ONCE] = pooled / total
    joined = jnp.concatenate(
        [
            pooled_ref[h * head_width : (h + 1) * head_width, h * tokens : (h + 1) * tokens]
            for h in range(HEADS)
        ],
        axis=0,
    ).T
    queries = layer_norm(queries + wide_mm(joined, t2i_out_ref[...]), gains_ref[1:2])
    hidden = jnp.maximum(wide_mm(queries, mlp_up_ref[...]), 0.0)
    queries = layer_norm(queries + wide_mm(hidden, mlp_down_ref[...]), gains_ref[2:3])

    back_k = wide_mm(queries + start, i2t_qkv_ref[:, inner : 2 * inner])
    back_v = wide_mm(queries, i2t_qkv_ref[:, 2 * inner :])
    gaps = by_group(back_k[:slots] - back_k[slots:], inner)
    gaps = wide_mm(gaps, i2t_qkv_ref[:, :inner], mm_t) * (0.5 * head_scale)
    gaps = gaps.astype(bf16)
    middle = 0.5 * (back_v[:slots] + back_v[slots:])
    apart = by_group(0.5 * (back_v[:slots] - back_v[slots:]), inner)
    moves = wide_mm(jnp.concatenate([apart, middle], axis=0), i2t_out_ref[...])
    moves = (moves - jnp.mean(moves, axis=1, keepdims=True)).astype(bf16)
    hyper = wide_mm(jnp.maximum(wide_mm(queries[:slots], hyper_ref[0]), 0.0), hyper_ref[1])
    hyper = hyper.astype(bf16).astype(f32) * gains_ref[3:4]
    hyper = (hyper - jnp.mean(hyper, axis=1, keepdims=True)).astype(bf16)
    apart, middle = moves[: HEADS * slots], moves[HEADS * slots :]
    middle_wide, hyper_wide = middle.astype(f32), hyper.astype(f32)
    consts = jnp.concatenate(
        [
            jnp.sum(middle_wide * middle_wide, axis=1, keepdims=True),
            jnp.sum(middle_wide * hyper_wide, axis=1, keepdims=True),
        ],
        axis=1,
    )
    block = HEADS * SLOT_GROUP
    tall = block + 2 * SLOT_GROUP
    row_slot = lax.rem(lax.broadcasted_iota(jnp.int32, (tall, block), 0), SLOT_GROUP)
    column_slot = lax.rem(lax.broadcasted_iota(jnp.int32, (tall, block), 1), SLOT_GROUP)
    on_cells, on_weights = [], []
    for at in range(0, slots, SLOT_GROUP):
        mine = apart[at * HEADS : (at + SLOT_GROUP) * HEADS]
        mine_twice = (2.0 * mine.astype(f32)).astype(bf16)
        centre_twice = (2.0 * middle_wide[at : at + SLOT_GROUP]).astype(bf16)
        mask = hyper[at : at + SLOT_GROUP]
        on_cells += [mine_twice, centre_twice, mask]
        crossed = mm_t(jnp.concatenate([mine, centre_twice, mask], axis=0), mine)
        on_weights.append(jnp.where(row_slot == column_slot, crossed, 0.0).astype(bf16))
    on_cells.append(jnp.ones((SLOT_GROUP, width), bf16))
    on_cells = jnp.concatenate(on_cells, axis=0)
    on_weights = jnp.concatenate(on_weights, axis=0)
    gaps_ref[...] = gaps
    on_cells_ref[...] = on_cells
    on_weights_ref[...] = on_weights
    consts_ref[...] = consts

    weights = cell_weights(gaps, seam_keys_ref[...].astype(bf16))
    _, covers = cell_logits(
        weights, seam_cells_ref[...].astype(bf16), on_cells, on_weights, consts, live
    )
    count = 2 * SEAM * side
    line = lax.broadcasted_iota(jnp.int32, (side, count), 0)
    column = lax.broadcasted_iota(jnp.int32, (side, count), 1)
    near = (column >= line * 2 * SEAM) & (column < (line + 1) * 2 * SEAM)
    ours = lax.rem(lax.broadcasted_iota(jnp.int32, (count, side), 0), 2 * SEAM)
    theirs = lax.broadcasted_iota(jnp.int32, (count, side), 1)
    left = jnp.where(ours < SEAM, SEAM + 1 - (side + ours - theirs), 0)
    right = jnp.where(ours >= SEAM, SEAM + 1 - (theirs + 2 * SEAM - ours), 0)
    lines = jnp.where(near, covers, 0.0)
    scale = 1.0 / (SEAM + 1) ** 2
    to_left_ref[...] = scale * wide_mm(lines, jnp.maximum(left, 0).astype(f32).astype(bf16))
    to_right_ref[...] = scale * wide_mm(lines, jnp.maximum(right, 0).astype(f32).astype(bf16))


def image_kernel(
    counts_ref,
    cells_ref,
    keys_ref,
    gaps_ref,
    on_cells_ref,
    on_weights_ref,
    consts_ref,
    logits_ref,
    blended_ref,
    coverage_ref,
):
    pixels, width = cells_ref.shape
    side = math.isqrt(pixels)
    live = counts_ref[0, lax.axis_index("row")]
    gaps, on_cells, on_weights = gaps_ref[...], on_cells_ref[...], on_weights_ref[...]
    consts = consts_ref[...]
    places = [slice(at, at + CELLS_AT_ONCE) for at in range(0, pixels, CELLS_AT_ONCE)]
    weights = cell_weights(gaps, keys_ref[places[0], :])
    for step, place in enumerate(places):
        now = weights
        if step + 1 < len(places):
            weights = cell_weights(gaps, keys_ref[places[step + 1], :])
        logits, covers = cell_logits(now, cells_ref[place, :], on_cells, on_weights, consts, live)
        logits_ref[:, place] = logits
        for at in range(0, CELLS_AT_ONCE, side):
            line = (step * CELLS_AT_ONCE + at) // side
            coverage_ref[line : line + 1, :] = covers[:, at : at + side]
    apart = jnp.abs(
        lax.broadcasted_iota(jnp.int32, (side, side), 0)
        - lax.broadcasted_iota(jnp.int32, (side, side), 1)
    )
    band = jnp.maximum(SEAM + 1 - apart, 0).astype(f32).astype(bf16)
    blended_ref[...] = (1.0 / (SEAM + 1) ** 2) * wide_mm(coverage_ref[...], band)


def shards(
    embedding,
    counts,
    points,
    pe_gauss,
    point_embed,
    mask_token,
    sa_qkv,
    sa_out,
    t2i_qkv,
    t2i_out,
    mlp_up,
    mlp_down,
    i2t_qkv,
    i2t_out,
    hyper_w,
    ln_gains,
):
    side = embedding.shape[0]
    width = embedding.shape[2]
    inner = t2i_qkv.shape[1] // 3
    slots = points.shape[3]
    pixels = side * side
    groups = slots // SLOT_GROUP
    tall = (HEADS + 2) * SLOT_GROUP
    whole = pl.BlockSpec(memory_space=pltpu.VMEM)
    scalars = pl.BlockSpec(memory_space=pltpu.SMEM)
    cells = embedding.reshape(pixels, width)
    shape = jax.ShapeDtypeStruct
    params = pltpu.CompilerParams(vmem_limit_bytes=58 << 20)
    *slot_side, to_left, to_right = pl.pallas_call(
        decode_kernel,
        out_shape=(
            shape((pixels, width), bf16),
            shape((HEADS * slots, width), bf16),
            shape((groups * tall + SLOT_GROUP, width), bf16),
            shape((groups * tall, HEADS * SLOT_GROUP), bf16),
            shape((slots, 2), f32),
            shape((side, side), f32),
            shape((side, side), f32),
        ),
        in_specs=[scalars] + [whole] * 15,
        out_specs=(whole,) * 7,
        scratch_shapes=[
            pltpu.VMEM((2 * SEAM * side, width), f32),
            pltpu.VMEM((2 * SEAM * side, width), f32),
            pltpu.VMEM((inner, pixels), bf16),
            pltpu.VMEM((inner, 2 * slots * HEADS), f32),
        ],
        compiler_params=params,
        name="decode",
    )(
        counts,
        points.reshape(2, slots),
        pe_gauss,
        point_embed.reshape(1, width),
        mask_token.reshape(1, width),
        sa_qkv,
        sa_out,
        t2i_qkv,
        t2i_out,
        mlp_up,
        mlp_down,
        i2t_qkv,
        i2t_out,
        hyper_w,
        ln_gains,
        cells,
    )
    count = lax.axis_size("col")
    from_right = lax.ppermute(to_left, "col", [(i + 1, i) for i in range(count - 1)])
    from_left = lax.ppermute(to_right, "col", [(i, i + 1) for i in range(count - 1)])
    logits, blended = pl.pallas_call(
        image_kernel,
        out_shape=(shape((slots, pixels), bf16), shape((side, side), f32)),
        in_specs=[scalars] + [whole] * 6,
        out_specs=(whole,) * 2,
        scratch_shapes=[pltpu.VMEM((side, side), f32)],
        compiler_params=params,
        name="image",
    )(counts, cells, *slot_side)
    return (logits.reshape(1, 1, slots, pixels), blended + from_left + from_right)


def solution(mesh):
    placed = (P("row", "col", None), P("col", None), P("row", "col", None, None)) + (P(),) * 13
    return jax.shard_map(
        shards,
        mesh=mesh,
        in_specs=placed,
        out_specs=(P("row", "col", None, None), P("row", "col")),
        check_vma=False,
    )
```

time: 36.3 us -> 33.5 us (0.923)
  waiting for transfers between devices: 4.51 us -> 0.01 us
  Pallas kernels: 23 us -> 24.8 us
  local copies, waits for them, and re-layouts: 0.86 us -> 0 us
  other arithmetic: 0.81 us -> 1.38 us
    ppermute x2, waiting for transfers between devices: 4.51 us -> 0.01 us  [the longest x1 0.01 us: shards(): lax.ppermute(to_right, 'col', [(i, i + 1) for i in range(count - 1)])]
    pallas_call x1 -> x2, Pallas kernels: 23 us -> 24.8 us  [the longest x1 17.1 us: shards(): pl.pallas_call(decode_kernel, out_shape=(shape((pixels, width), bf16), sh...]
    reshape x1 -> x0, local copies, waits for them, and re-layouts: 0.79 us -> none  [shards(): coverage = coverage.reshape(side, side)]
    add x1, other arithmetic: 0.81 us -> 1.38 us  [shards(): blended + from_left + from_right]
  transfers between devices with their start and end apart: 2 -> 2, of which waited for: 2 -> 0; matrix products, arithmetic and copies ran while one was open for 0% -> 0% of each run, Pallas kernels for 0% -> 23%
where the time goes in v2:
time: 33.5 us; the launch traced here: 33.2 us
  Pallas kernels  24.8 us (74%)
  starting transfers between devices  6.42 us (19%)
  other arithmetic  1.38 us (4%)
  between operations  0.66 us (2%)
    pallas_call x1, Pallas kernels, shards(): pl.pallas_call(decode_kernel, out_shape=(shape((pixels, width), bf16), sh...  17.1 us
    pallas_call x1, Pallas kernels, shards(): pl.pallas_call(image_kernel, out_shape=(shape((slots, pixels), bf16), sha...  7.7 us
    ppermute x1, starting transfers between devices, shards(): lax.ppermute(to_right, 'col', [(i, i + 1) for i in range(count - 1)])  4.94 us
    ppermute x1, starting transfers between devices, shards(): lax.ppermute(to_left, 'col', [(i + 1, i) for i in range(count - 1)])  1.47 us
    add x1, other arithmetic, shards(): blended + from_left + from_right  1.38 us
  transfers between devices with their start and end apart: 2, of which 0 were waited for; matrix products, arithmetic and copies ran while one was open for 0% of the time, Pallas kernels for 23%

profile of v2, /device:TPU:0, one launch (start us, length us, event | category | flops | bytes accessed | tf_op | source)
XLA Modules:
  0.0 33.2 jit_solution(11829872978586523542)
XLA Ops:
  0.6 17.1 %decode.1 = (bf16[4096,256]{1,0:T(8,128)(2,1)}, bf16[384,256]{1,0:T(8,128)(2,1)}, bf16[496,256]{1,0:T(8,128)(2,1)}, bf16[480,128]{1,0:T(8,128)(2,1)}, f32[48,2]{...) custom-call(s32[1,8]{1,0:T(1,128)} %counts_ref.3, s32[2,48]{1,0:T(2,128)} %bitcast.7, f32[2,128]{1,0:T(2,128)} %gauss_ref.1, ...), custom_call_target="tpu_custom_call" | custom-call | tf_op jit(solution)/shard_map/decode/pallas_call | solution.py:380
  17.7 4.9 %collective-permute-start = (f32[64,64]{1,0:T(8,128)}, f32[64,64]{1,0:T(8,128)S(1)}, u32[]{:S(2)}, u32[]{:S(2)}) collective-permute-start(f32[64,64]{1,0:T(8,128)} %get-tuple-element.18), channel_id=1, source_target_pairs={{0,1},{1,2},{2,3},{4,5},{5,6},{6,7},{8,9},{9,10},{10,11},{12,13},{... | collective-permute-start | bytes 49160 | tf_op jit(solution)/shard_map/ppermute | solution.py:421
  22.6 1.5 %collective-permute-start.1 = (f32[64,64]{1,0:T(8,128)}, f32[64,64]{1,0:T(8,128)S(1)}, u32[]{:S(2)}, u32[]{:S(2)}) collective-permute-start(f32[64,64]{1,0:T(8,128)} %get-tuple-element.19), channel_id=1, source_target_pairs={{1,0},{2,1},{3,2},{5,4},{6,5},{7,6},{9,8},{10,9},{11,10},{13,12},{... | collective-permute-start | bytes 49160 | tf_op jit(solution)/shard_map/ppermute | solution.py:420
  24.1 7.7 %image.1 = (bf16[48,4096]{1,0:T(8,128)(2,1)}, f32[64,64]{1,0:T(8,128)}) custom-call(s32[1,8]{1,0:T(1,128)} %counts_ref.3, bf16[4096,256]{1,0:T(8,128)(2,1)} %bitcast.6, bf16[4096,256]{1,0:T(8,128)(2,1)} %get-tuple-element.11.keys_ref, bf16[384,256]{1,0:T(8,128)(2,1)} %get-tuple-element.12.gaps_ref, bf16[496,256]{1,0:T(8,128)(2,1)} %get-tuple-element.13.on_cells_ref, ...), custom_call_target="tpu_custom_call" | custom-call | tf_op jit(solution)/shard_map/image/pallas_call | solution.py:422
  31.8 0.0 collective-permute-done
  31.8 0.0 collective-permute-done.1
  31.8 1.4 %add_add_fusion = f32[64,64]{1,0:T(8,128)} fusion(f32[64,64]{1,0:T(8,128)S(1)} %collective-permute-done.1, f32[64,64]{1,0:T(8,128)} %get-tuple-element.17, f32[64,64]{1,0:T(8,128)S(1)} %collective-permute-done), kind=kLoop, calls=%fused_computation | loop fusion | flops 8192 | bytes 65536 | tf_op jit(solution)/shard_map/add | solution.py:431
Async XLA Ops:
  17.7 14.1 %collective-permute-start = (f32[64,64]{1,0:T(8,128)}, f32[64,64]{1,0:T(8,128)S(1)}, u32[]{:S(2)}, u32[]{:S(2)}) collective-permute-start(f32[64,64]{1,0:T(8,128)} %get-tuple-element.18), channel_id=1, source_target_pairs={{0,1},{1,2},{2,3},{4,5},{5,6},{6,7},{8,9},{9,10},{10,11},{12,13},{... | collective-permute-start | bytes 49160 | tf_op jit(solution)/shard_map/ppermute | solution.py:421
  22.6 9.2 %collective-permute-start.1 = (f32[64,64]{1,0:T(8,128)}, f32[64,64]{1,0:T(8,128)S(1)}, u32[]{:S(2)}, u32[]{:S(2)}) collective-permute-start(f32[64,64]{1,0:T(8,128)} %get-tuple-element.19), channel_id=1, source_target_pairs={{1,0},{2,1},{3,2},{5,4},{6,5},{7,6},{9,8},{10,9},{11,10},{13,12},{... | collective-permute-start | bytes 49160 | tf_op jit(solution)/shard_map/ppermute | solution.py:420

commit v3 on v2

--- a/solution.py
+++ b/solution.py
@@ -12,8 +12,11 @@
 SEAM = 4
 IMG = 1024
 SLOT_GROUP = 16
-KEYS_AT_ONCE = 1024
+KEYS_AT_ONCE = 512
 PROBES_AT_ONCE = 256
+FOLD = 64
+ARRAYS = 16
+FETCH_ORDER = (2, 1, 4, 3, 14, 5, 6, 7, 15, 8, 9, 10, 11, 12, 13, 0)
 CELLS_AT_ONCE = 512
 
 norm_eps = 1e-05
@@ -57,6 +60,17 @@
         sign = 1.0 if order % 4 == 1 else -1.0
         total = total * square + sign / math.factorial(order)
     return total * angle
+
+
+def fold_rows(values, join):
+    total = values[:FOLD]
+    for at in range(FOLD, values.shape[0], FOLD):
+        total = join(total, values[at : at + FOLD])
+    rows = FOLD
+    while rows > 1:
+        rows //= 2
+        total = join(total[:rows], total[rows:])
+    return total
 
 
 def by_head(rows, inner_width):
@@ -122,7 +136,19 @@
     return jnp.concatenate(logits, axis=0), jnp.sum(sum(covers), axis=0, keepdims=True)
 
 
-def decode_kernel(
+def decode_kernel(*refs):
+    far, refs = refs[:ARRAYS], refs[ARRAYS:]
+    (cells_ref, *slot_side), refs = refs[:8], refs[8:]
+    near, (sems, *scratch) = refs[: ARRAYS - 1], refs[ARRAYS - 1 :]
+    near = [*near, cells_ref]
+    copies = [pltpu.make_async_copy(*pair, sems.at[at]) for at, pair in enumerate(zip(far, near))]
+    for at in FETCH_ORDER:
+        copies[at].start()
+    decode(copies, *near, *slot_side, *scratch)
+
+
+def decode(
+    copies,
     counts_ref,
     points_ref,
     gauss_ref,
@@ -144,8 +170,8 @@
     on_cells_ref,
     on_weights_ref,
     consts_ref,
-    to_left_ref,
-    to_right_ref,
+    even_ref,
+    odd_ref,
     seam_cells_ref,
     seam_keys_ref,
     values_ref,
@@ -157,7 +183,8 @@
     inner = t2i_qkv_ref.shape[1] // 3
     head_width = inner // HEADS
     half = width // 2
-    live = counts_ref[0, lax.axis_index("row")]
+    for at in FETCH_ORDER[:5]:
+        copies[at].wait()
 
     gauss = gauss_ref[...]
     steps = lax.broadcasted_iota(jnp.int32, (side, half), 0).astype(f32)
@@ -183,6 +210,8 @@
         ],
         axis=0,
     )
+    for at in FETCH_ORDER[5:8]:
+        copies[at].wait()
     qkv = wide_mm(start, sa_qkv_ref[...])
     query, key, value = qkv[:, :width], qkv[:, width : 2 * width], qkv[:, 2 * width :]
     key_gap = key[:slots] - key[slots:]
@@ -201,6 +230,7 @@
     probes = mm_t(cross_q, t2i_qkv_ref[:, inner : 2 * inner]) * (head_scale * math.log2(math.e))
     probes = probes.astype(bf16)
 
+    copies[FETCH_ORDER[8]].wait()
     sin_x, cos_x = sines[:side], cosines[:side]
     left_half = lax.broadcasted_iota(jnp.int32, (2 * SEAM, width), 0) < SEAM
     for line in range(side):
@@ -220,26 +250,35 @@
         t2i_qkv_ref[:, 2 * inner :].astype(f32).T.astype(bf16), cells_ref[...]
     ).astype(bf16)
     tokens = start.shape[0]
-    for at in range(0, HEADS * tokens, PROBES_AT_ONCE):
-        probe = probes[at : at + PROBES_AT_ONCE]
-        rows = slice(
-            at // tokens * head_width, ((at + PROBES_AT_ONCE - 1) // tokens + 1) * head_width
-        )
-        for cell in range(0, pixels, KEYS_AT_ONCE):
-            near = slice(cell, cell + KEYS_AT_ONCE)
-            raw = mm_t(keys_ref[near, :], probe)
-            top = jnp.max(raw, axis=0, keepdims=True)
+    def raw_scores(cell):
+        return mm_t(keys_ref[cell : cell + KEYS_AT_ONCE, :], probes)
+
+    ahead = raw_scores(0)
+    for cell in range(0, pixels, KEYS_AT_ONCE):
+        raw = ahead
+        if cell + KEYS_AT_ONCE < pixels:
+            ahead = raw_scores(cell + KEYS_AT_ONCE)
+        top = fold_rows(raw, jnp.maximum)
+        if cell > 0:
+            top = jnp.maximum(top, old_top)
+            fade = jnp.exp2(old_top - top)
+        raw = jnp.exp2(raw - top)
+        total = fold_rows(raw, jnp.add)
+        raw = raw.astype(bf16)
+        if cell > 0:
+            total = total + fade * old_total
+        for at in range(0, HEADS * tokens, PROBES_AT_ONCE):
+            rows = slice(
+                at // tokens * head_width, ((at + PROBES_AT_ONCE - 1) // tokens + 1) * head_width
+            )
+            lanes = slice(at, at + PROBES_AT_ONCE)
+            pooled = mm(values_ref[rows, cell : cell + KEYS_AT_ONCE], raw[:, lanes])
             if cell > 0:
-                top = jnp.maximum(top, old_top)
-                fade = jnp.exp2(old_top - top)
-            raw = jnp.exp2(raw - top)
-            total = jnp.sum(raw, axis=0, keepdims=True)
-            pooled = mm(values_ref[rows, near], raw.astype(bf16))
-            if cell > 0:
-                total = total + fade * old_total
-                pooled = pooled + fade * old_pooled
-            old_top, old_total, old_pooled = top, total, pooled
-        pooled_ref[rows, at : at + PROBES_AT_ONCE] = pooled / total
+                pooled = pooled + fade[:, lanes] * pooled_ref[rows, lanes]
+            if cell + KEYS_AT_ONCE == pixels:
+                pooled = pooled / total[:, lanes]
+            pooled_ref[rows, lanes] = pooled
+        old_top, old_total = top, total
     joined = jnp.concatenate(
         [
             pooled_ref[h * head_width : (h + 1) * head_width, h * tokens : (h + 1) * tokens]
@@ -247,6 +286,8 @@
         ],
         axis=0,
     ).T
+    for at in FETCH_ORDER[9:]:
+        copies[at].wait()
     queries = layer_norm(queries + wide_mm(joined, t2i_out_ref[...]), gains_ref[1:2])
     hidden = jnp.maximum(wide_mm(queries, mlp_up_ref[...]), 0.0)
     queries = layer_norm(queries + wide_mm(hidden, mlp_down_ref[...]), gains_ref[2:3])
@@ -293,6 +334,7 @@
     on_weights_ref[...] = on_weights
     consts_ref[...] = consts
 
+    live = counts_ref[0, lax.axis_index("row")]
     weights = cell_weights(gaps, seam_keys_ref[...].astype(bf16))
     _, covers = cell_logits(
         weights, seam_cells_ref[...].astype(bf16), on_cells, on_weights, consts, live
@@ -307,8 +349,11 @@
     right = jnp.where(ours >= SEAM, SEAM + 1 - (theirs + 2 * SEAM - ours), 0)
     lines = jnp.where(near, covers, 0.0)
     scale = 1.0 / (SEAM + 1) ** 2
-    to_left_ref[...] = scale * wide_mm(lines, jnp.maximum(left, 0).astype(f32).astype(bf16))
-    to_right_ref[...] = scale * wide_mm(lines, jnp.maximum(right, 0).astype(f32).astype(bf16))
+    to_left = scale * wide_mm(lines, jnp.maximum(left, 0).astype(f32).astype(bf16))
+    to_right = scale * wide_mm(lines, jnp.maximum(right, 0).astype(f32).astype(bf16))
+    even = lax.rem(lax.axis_index("col"), 2) == 0
+    even_ref[...] = jnp.where(even, to_right, to_left)
+    odd_ref[...] = jnp.where(even, to_left, to_right)
 
 
 def image_kernel(
@@ -322,6 +367,8 @@
     logits_ref,
     blended_ref,
     coverage_ref,
+    found_ref,
+    sems,
 ):
     pixels, width = cells_ref.shape
     side = math.isqrt(pixels)
@@ -330,12 +377,17 @@
     consts = consts_ref[...]
     places = [slice(at, at + CELLS_AT_ONCE) for at in range(0, pixels, CELLS_AT_ONCE)]
     weights = cell_weights(gaps, keys_ref[places[0], :])
+    copies = []
     for step, place in enumerate(places):
         now = weights
         if step + 1 < len(places):
             weights = cell_weights(gaps, keys_ref[places[step + 1], :])
         logits, covers = cell_logits(now, cells_ref[place, :], on_cells, on_weights, consts, live)
-        logits_ref[:, place] = logits
+        found_ref[:, place] = logits
+        copies.append(
+            pltpu.make_async_copy(found_ref.at[:, place], logits_ref.at[:, place], sems.at[step])
+        )
+        copies[-1].start()
         for at in range(0, CELLS_AT_ONCE, side):
             line = (step * CELLS_AT_ONCE + at) // side
             coverage_ref[line : line + 1, :] = covers[:, at : at + side]
@@ -345,6 +397,8 @@
     )
     band = jnp.maximum(SEAM + 1 - apart, 0).astype(f32).astype(bf16)
     blended_ref[...] = (1.0 / (SEAM + 1) ** 2) * wide_mm(coverage_ref[...], band)
+    for copy in copies:
+        copy.wait()
 
 
 def shards(
@@ -376,10 +430,33 @@
     scalars = pl.BlockSpec(memory_space=pltpu.SMEM)
     cells = embedding.reshape(pixels, width)
     shape = jax.ShapeDtypeStruct
-    params = pltpu.CompilerParams(vmem_limit_bytes=58 << 20)
-    *slot_side, to_left, to_right = pl.pallas_call(
+    params = pltpu.CompilerParams(vmem_limit_bytes=36 << 20)
+    far = pl.BlockSpec(memory_space=pltpu.HBM)
+    arrays = [
+        pltpu.with_memory_space_constraint(one, pltpu.HBM)
+        for one in (
+            counts,
+            points.reshape(2, slots),
+            pe_gauss,
+            point_embed.reshape(1, width),
+            mask_token.reshape(1, width),
+            sa_qkv,
+            sa_out,
+            t2i_qkv,
+            t2i_out,
+            mlp_up,
+            mlp_down,
+            i2t_qkv,
+            i2t_out,
+            hyper_w,
+            ln_gains,
+            cells,
+        )
+    ]
+    *slot_side, even, odd = pl.pallas_call(
         decode_kernel,
         out_shape=(
+            shape((pixels, width), bf16),
             shape((pixels, width), bf16),
             shape((HEADS * slots, width), bf16),
             shape((groups * tall + SLOT_GROUP, width), bf16),
@@ -388,9 +465,12 @@
             shape((side, side), f32),
             shape((side, side), f32),
         ),
-        in_specs=[scalars] + [whole] * 15,
-        out_specs=(whole,) * 7,
-        scratch_shapes=[
+        in_specs=[far] * ARRAYS,
+        out_specs=(whole,) * 8,
+        scratch_shapes=[pltpu.SMEM(counts.shape, counts.dtype)]
+        + [pltpu.VMEM(one.shape, one.dtype) for one in arrays[1:-1]]
+        + [
+            pltpu.SemaphoreType.DMA((ARRAYS,)),
             pltpu.VMEM((2 * SEAM * side, width), f32),
             pltpu.VMEM((2 * SEAM * side, width), f32),
             pltpu.VMEM((inner, pixels), bf16),
@@ -398,37 +478,28 @@
         ],
         compiler_params=params,
         name="decode",
-    )(
-        counts,
-        points.reshape(2, slots),
-        pe_gauss,
-        point_embed.reshape(1, width),
-        mask_token.reshape(1, width),
-        sa_qkv,
-        sa_out,
-        t2i_qkv,
-        t2i_out,
-        mlp_up,
-        mlp_down,
-        i2t_qkv,
-        i2t_out,
-        hyper_w,
-        ln_gains,
-        cells,
-    )
+    )(*arrays)
     count = lax.axis_size("col")
-    from_right = lax.ppermute(to_left, "col", [(i + 1, i) for i in range(count - 1)])
-    from_left = lax.ppermute(to_right, "col", [(i, i + 1) for i in range(count - 1)])
+    swaps = [
+        [pair for i in range(first, count - 1, 2) for pair in ((i, i + 1), (i + 1, i))]
+        for first in (0, 1)
+    ]
+    odd = lax.ppermute(odd, "col", swaps[1])
+    even = lax.ppermute(even, "col", swaps[0])
     logits, blended = pl.pallas_call(
         image_kernel,
         out_shape=(shape((slots, pixels), bf16), shape((side, side), f32)),
         in_specs=[scalars] + [whole] * 6,
-        out_specs=(whole,) * 2,
-        scratch_shapes=[pltpu.VMEM((side, side), f32)],
+        out_specs=(pl.BlockSpec(memory_space=pltpu.HBM), whole),
+        scratch_shapes=[
+            pltpu.VMEM((side, side), f32),
+            pltpu.VMEM((slots, pixels), bf16),
+            pltpu.SemaphoreType.DMA((pixels // CELLS_AT_ONCE,)),
+        ],
         compiler_params=params,
         name="image",
-    )(counts, cells, *slot_side)
-    return (logits.reshape(1, 1, slots, pixels), blended + from_left + from_right)
+    )(arrays[0], *slot_side)
+    return (logits.reshape(1, 1, slots, pixels), blended + odd + even)
 
 
 def solution(mesh):

time: 33.5 us -> 24.6 us (0.73)
  Pallas kernels: 24.8 us -> 16.6 us
  other arithmetic: 1.38 us -> 0.62 us
    pallas_call x1, Pallas kernels: 17.1 us -> 10.6 us  [shards(): pl.pallas_call(decode_kernel, out_shape=(shape((pixels, width), bf16), sh...]
    pallas_call x1, Pallas kernels: 7.7 us -> 5.98 us  [shards(): pl.pallas_call(image_kernel, out_shape=(shape((slots, pixels), bf16), sha...]
    add x1, other arithmetic: 1.38 us -> 0.62 us  [shards(): return (logits.reshape(1, 1, slots, pixels), blended + odd + even)]
  transfers between devices with their start and end apart: 2 -> 2, of which waited for: 0 -> 0; matrix products, arithmetic and copies ran while one was open for 0% -> 0% of each run, Pallas kernels for 23% -> 24%
where the time goes in v3:
time: 24.6 us; the launch traced here: 24.5 us
  Pallas kernels  16.6 us (67%)
  starting transfers between devices  6.6 us (27%)
  between operations  0.68 us (3%)
  other arithmetic  0.62 us (3%)
    pallas_call x1, Pallas kernels, shards(): pl.pallas_call(decode_kernel, out_shape=(shape((pixels, width), bf16), sh...  10.6 us
    pallas_call x1, Pallas kernels, shards(): pl.pallas_call(image_kernel, out_shape=(shape((slots, pixels), bf16), sha...  5.98 us
    ppermute x1, starting transfers between devices, shards(): even = lax.ppermute(even, 'col', swaps[0])  5.94 us
    ppermute x1, starting transfers between devices, shards(): odd = lax.ppermute(odd, 'col', swaps[1])  0.66 us
    add x1, other arithmetic, shards(): return (logits.reshape(1, 1, slots, pixels), blended + odd + even)  0.62 us
  transfers between devices with their start and end apart: 2, of which 0 were waited for; matrix products, arithmetic and copies ran while one was open for 0% of the time, Pallas kernels for 24%

profile of v3, /device:TPU:0, one launch (start us, length us, event | category | flops | bytes accessed | tf_op | source)
XLA Modules:
  0.0 24.5 jit_solution(11597247364017668602)
XLA Ops:
  0.6 10.6 %decode.1 = (bf16[4096,256]{1,0:T(8,128)(2,1)S(1)}, bf16[4096,256]{1,0:T(8,128)(2,1)S(1)}, bf16[384,256]{1,0:T(8,128)(2,1)S(1)}, bf16[496,256]{1,0:T(8,128)(2,1)...) custom-call(s32[1,8]{1,0:T(1,128)} %counts_ref.1, ...), custom_call_target="tpu_custom_call" | custom-call | tf_op jit(solution)/shard_map/decode/pallas_call | solution.py:456
  11.2 0.7 %collective-permute-start = (f32[64,64]{1,0:T(8,128)S(1)}, f32[64,64]{1,0:T(8,128)S(1)}, u32[]{:S(2)}, u32[]{:S(2)}) collective-permute-start(f32[64,64]{1,0:T(8,128)S(1)} %get-tuple-element.20), channel_id=1, source_target_pairs={{1,2},{2,1},{5,6},{6,5},{9,10},{10,9},{13,14},{14,13},{17,18},{18,... | collective-permute-start | bytes 49160 | tf_op jit(solution)/shard_map/ppermute | solution.py:487
  11.9 5.9 %collective-permute-start.1 = (f32[64,64]{1,0:T(8,128)S(1)}, f32[64,64]{1,0:T(8,128)S(1)}, u32[]{:S(2)}, u32[]{:S(2)}) collective-permute-start(f32[64,64]{1,0:T(8,128)S(1)} %get-tuple-element.21), channel_id=1, source_target_pairs={{0,1},{1,0},{2,3},{3,2},{4,5},{5,4},{6,7},{7,6},{8,9},{9,8},{10,11... | collective-permute-start | bytes 49160 | tf_op jit(solution)/shard_map/ppermute | solution.py:488
  17.8 6.0 %image.1 = (bf16[48,4096]{1,0:T(8,128)(2,1)}, f32[64,64]{1,0:T(8,128)S(1)}) custom-call(s32[1,8]{1,0:T(1,128)} %counts_ref.1, bf16[4096,256]{1,0:T(8,128)(2,1)S(1)} %get-tuple-element.12.cells_ref, bf16[4096,256]{1,0:T(8,128)(2,1)S(1)} %get-tuple-element.13.keys_ref, bf16[384,256]{1,0:T(8,128)(2,1)S(1)} %get-tuple-element.14.gaps_ref, ...), custom_call_target="tpu_custom_call" | custom-call | tf_op jit(solution)/shard_map/image/pallas_call | solution.py:489
  23.8 0.0 collective-permute-done
  23.8 0.0 collective-permute-done.1
  23.8 0.6 %add_add_fusion = f32[64,64]{1,0:T(8,128)} fusion(f32[64,64]{1,0:T(8,128)S(1)} %collective-permute-done.1, f32[64,64]{1,0:T(8,128)S(1)} %get-tuple-element.19, f32[64,64]{1,0:T(8,128)S(1)} %collective-permute-done), kind=kLoop, calls=%fused_computation | loop fusion | flops 8192 | bytes 65536 | tf_op jit(solution)/shard_map/add | solution.py:502
Async XLA Ops:
  11.2 12.6 %collective-permute-start = (f32[64,64]{1,0:T(8,128)S(1)}, f32[64,64]{1,0:T(8,128)S(1)}, u32[]{:S(2)}, u32[]{:S(2)}) collective-permute-start(f32[64,64]{1,0:T(8,128)S(1)} %get-tuple-element.20), channel_id=1, source_target_pairs={{1,2},{2,1},{5,6},{6,5},{9,10},{10,9},{13,14},{14,13},{17,18},{18,... | collective-permute-start | bytes 49160 | tf_op jit(solution)/shard_map/ppermute | solution.py:487
  11.9 11.9 %collective-permute-start.1 = (f32[64,64]{1,0:T(8,128)S(1)}, f32[64,64]{1,0:T(8,128)S(1)}, u32[]{:S(2)}, u32[]{:S(2)}) collective-permute-start(f32[64,64]{1,0:T(8,128)S(1)} %get-tuple-element.21), channel_id=1, source_target_pairs={{0,1},{1,0},{2,3},{3,2},{4,5},{5,4},{6,7},{7,6},{8,9},{9,8},{10,11... | collective-permute-start | bytes 49160 | tf_op jit(solution)/shard_map/ppermute | solution.py:488

commit v4 on v3

--- a/solution.py
+++ b/solution.py
@@ -44,6 +44,10 @@
     return both[:rows] + both[rows:]
 
 
+def token_mm(values, weight):
+    return mm(values.astype(bf16), weight)
+
+
 def layer_norm(values, gain):
     centred = values - jnp.mean(values, axis=-1, keepdims=True)
     spread = jnp.mean(centred * centred, axis=-1, keepdims=True)
@@ -113,9 +117,20 @@
     tall = block + 2 * SLOT_GROUP
     flat = mm_t(on_cells, cells)
     wide = cells.astype(f32)
-    norms = mm_t(jnp.ones((SLOT_GROUP, width), bf16), halves(wide * wide))
+    norms = jnp.sum(wide * wide, axis=1, keepdims=True)
+    lanes = 128
+    same = lax.broadcasted_iota(jnp.int32, (lanes, lanes), 0) == lax.broadcasted_iota(
+        jnp.int32, (lanes, lanes), 1
+    )
+    norms = jnp.concatenate(
+        [
+            jnp.sum(jnp.where(same, norms[at : at + lanes], 0.0), axis=0, keepdims=True)
+            for at in range(0, count, lanes)
+        ],
+        axis=1,
+    )
     total = flat[slots // SLOT_GROUP * tall :][:SLOT_GROUP]
-    norms = norms[:, :count] + norms[:, count:] - total * total * (1.0 / width)
+    norms = norms - total * total * (1.0 / width)
     logits, covers = [], []
     for at in range(0, slots, SLOT_GROUP):
         group = at // SLOT_GROUP
@@ -289,8 +304,8 @@
     for at in FETCH_ORDER[9:]:
         copies[at].wait()
     queries = layer_norm(queries + wide_mm(joined, t2i_out_ref[...]), gains_ref[1:2])
-    hidden = jnp.maximum(wide_mm(queries, mlp_up_ref[...]), 0.0)
-    queries = layer_norm(queries + wide_mm(hidden, mlp_down_ref[...]), gains_ref[2:3])
+    hidden = jnp.maximum(token_mm(queries, mlp_up_ref[...]), 0.0)
+    queries = layer_norm(queries + token_mm(hidden, mlp_down_ref[...]), gains_ref[2:3])
 
     back_k = wide_mm(queries + start, i2t_qkv_ref[:, inner : 2 * inner])
     back_v = wide_mm(queries, i2t_qkv_ref[:, 2 * inner :])
@@ -499,7 +514,7 @@
         compiler_params=params,
         name="image",
     )(arrays[0], *slot_side)
-    return (logits.reshape(1, 1, slots, pixels), blended + odd + even)
+    return (logits.reshape(1, 1, slots, pixels), blended + even + odd)
 
 
 def solution(mesh):

time: 24.6 us -> 22 us (0.89)
  the two profiles are of different devices: /device:TPU:0 before, /device:TPU:14 now
where the time goes in v4:
time: 22 us; the launch traced here: 21.9 us
  Pallas kernels  15.4 us (70%)
  starting transfers between devices  5.12 us (23%)
  between operations  0.68 us (3%)
  other arithmetic  0.62 us (3%)
    pallas_call x1, Pallas kernels, shards(): pl.pallas_call(decode_kernel, out_shape=(shape((pixels, width), bf16), sh...  10.1 us
    pallas_call x1, Pallas kernels, shards(): pl.pallas_call(image_kernel, out_shape=(shape((slots, pixels), bf16), sha...  5.36 us
    ppermute x1, starting transfers between devices, shards(): odd = lax.ppermute(odd, 'col', swaps[1])  4.6 us
    add x1, other arithmetic, shards(): return (logits.reshape(1, 1, slots, pixels), blended + even + odd)  0.62 us
    ppermute x1, starting transfers between devices, shards(): even = lax.ppermute(even, 'col', swaps[0])  0.51 us
  transfers between devices with their start and end apart: 2, of which 0 were waited for; matrix products, arithmetic and copies ran while one was open for 0% of the time, Pallas kernels for 24%

profile of v4, /device:TPU:14, one launch (start us, length us, event | category | flops | bytes accessed | tf_op | source)
XLA Modules:
  0.0 21.9 jit_solution(16404404523239080257)
XLA Ops:
  0.6 10.1 %decode.1 = (bf16[4096,256]{1,0:T(8,128)(2,1)S(1)}, bf16[4096,256]{1,0:T(8,128)(2,1)S(1)}, bf16[384,256]{1,0:T(8,128)(2,1)S(1)}, bf16[496,256]{1,0:T(8,128)(2,1)...) custom-call(s32[1,8]{1,0:T(1,128)} %counts_ref.1, ...), custom_call_target="tpu_custom_call" | custom-call | tf_op jit(solution)/shard_map/decode/pallas_call | solution.py:471
  10.7 0.5 %collective-permute-start = (f32[64,64]{1,0:T(8,128)S(1)}, f32[64,64]{1,0:T(8,128)S(1)}, u32[]{:S(2)}, u32[]{:S(2)}) collective-permute-start(f32[64,64]{1,0:T(8,128)S(1)} %get-tuple-element.20), channel_id=1, source_target_pairs={{0,1},{1,0},{2,3},{3,2},{4,5},{5,4},{6,7},{7,6},{8,9},{9,8},{10,11... | collective-permute-start | bytes 49160 | tf_op jit(solution)/shard_map/ppermute | solution.py:503
  11.2 4.6 %collective-permute-start.1 = (f32[64,64]{1,0:T(8,128)S(1)}, f32[64,64]{1,0:T(8,128)S(1)}, u32[]{:S(2)}, u32[]{:S(2)}) collective-permute-start(f32[64,64]{1,0:T(8,128)S(1)} %get-tuple-element.21), channel_id=1, source_target_pairs={{1,2},{2,1},{5,6},{6,5},{9,10},{10,9},{13,14},{14,13},{17,18},{18,... | collective-permute-start | bytes 49160 | tf_op jit(solution)/shard_map/ppermute | solution.py:502
  15.9 5.4 %image.1 = (bf16[48,4096]{1,0:T(8,128)(2,1)}, f32[64,64]{1,0:T(8,128)S(1)}) custom-call(s32[1,8]{1,0:T(1,128)} %counts_ref.1, bf16[4096,256]{1,0:T(8,128)(2,1)S(1)} %get-tuple-element.12.cells_ref, bf16[4096,256]{1,0:T(8,128)(2,1)S(1)} %get-tuple-element.13.keys_ref, bf16[384,256]{1,0:T(8,128)(2,1)S(1)} %get-tuple-element.14.gaps_ref, ...), custom_call_target="tpu_custom_call" | custom-call | tf_op jit(solution)/shard_map/image/pallas_call | solution.py:504
  21.2 0.0 collective-permute-done
  21.2 0.0 collective-permute-done.1
  21.2 0.6 %add_add_fusion = f32[64,64]{1,0:T(8,128)} fusion(f32[64,64]{1,0:T(8,128)S(1)} %collective-permute-done.1, f32[64,64]{1,0:T(8,128)S(1)} %get-tuple-element.19, f32[64,64]{1,0:T(8,128)S(1)} %collective-permute-done), kind=kLoop, calls=%fused_computation | loop fusion | flops 8192 | bytes 65536 | tf_op jit(solution)/shard_map/add | solution.py:517
Async XLA Ops:
  10.7 10.5 %collective-permute-start = (f32[64,64]{1,0:T(8,128)S(1)}, f32[64,64]{1,0:T(8,128)S(1)}, u32[]{:S(2)}, u32[]{:S(2)}) collective-permute-start(f32[64,64]{1,0:T(8,128)S(1)} %get-tuple-element.20), channel_id=1, source_target_pairs={{0,1},{1,0},{2,3},{3,2},{4,5},{5,4},{6,7},{7,6},{8,9},{9,8},{10,11... | collective-permute-start | bytes 49160 | tf_op jit(solution)/shard_map/ppermute | solution.py:503
  11.2 10.0 %collective-permute-start.1 = (f32[64,64]{1,0:T(8,128)S(1)}, f32[64,64]{1,0:T(8,128)S(1)}, u32[]{:S(2)}, u32[]{:S(2)}) collective-permute-start(f32[64,64]{1,0:T(8,128)S(1)} %get-tuple-element.21), channel_id=1, source_target_pairs={{1,2},{2,1},{5,6},{6,5},{9,10},{10,9},{13,14},{14,13},{17,18},{18,... | collective-permute-start | bytes 49160 | tf_op jit(solution)/shard_map/ppermute | solution.py:502

commit v5 on v4

--- a/solution.py
+++ b/solution.py
@@ -12,9 +12,10 @@
 SEAM = 4
 IMG = 1024
 SLOT_GROUP = 16
-KEYS_AT_ONCE = 512
+KEYS_AT_ONCE = 1024
 PROBES_AT_ONCE = 256
 FOLD = 64
+IN_RANGE = 2.0**96
 ARRAYS = 16
 FETCH_ORDER = (2, 1, 4, 3, 14, 5, 6, 7, 15, 8, 9, 10, 11, 12, 13, 0)
 CELLS_AT_ONCE = 512
@@ -265,35 +266,57 @@
         t2i_qkv_ref[:, 2 * inner :].astype(f32).T.astype(bf16), cells_ref[...]
     ).astype(bf16)
     tokens = start.shape[0]
+    ones = jnp.ones((head_width, KEYS_AT_ONCE), bf16)
+    tiles = []
+    for at in range(0, HEADS * tokens, PROBES_AT_ONCE):
+        rows = slice(
+            at // tokens * head_width, ((at + PROBES_AT_ONCE - 1) // tokens + 1) * head_width
+        )
+        tiles.append((rows, slice(at, at + PROBES_AT_ONCE)))
+
     def raw_scores(cell):
         return mm_t(keys_ref[cell : cell + KEYS_AT_ONCE, :], probes)
 
+    def pool(cell, rows, share):
+        near = values_ref[rows, cell : cell + KEYS_AT_ONCE]
+        return mm(jnp.concatenate([near, ones], axis=0), share)
+
+    sums = [0.0] * len(tiles)
     ahead = raw_scores(0)
     for cell in range(0, pixels, KEYS_AT_ONCE):
         raw = ahead
         if cell + KEYS_AT_ONCE < pixels:
             ahead = raw_scores(cell + KEYS_AT_ONCE)
-        top = fold_rows(raw, jnp.maximum)
-        if cell > 0:
-            top = jnp.maximum(top, old_top)
-            fade = jnp.exp2(old_top - top)
-        raw = jnp.exp2(raw - top)
-        total = fold_rows(raw, jnp.add)
-        raw = raw.astype(bf16)
-        if cell > 0:
-            total = total + fade * old_total
-        for at in range(0, HEADS * tokens, PROBES_AT_ONCE):
-            rows = slice(
-                at // tokens * head_width, ((at + PROBES_AT_ONCE - 1) // tokens + 1) * head_width
-            )
-            lanes = slice(at, at + PROBES_AT_ONCE)
-            pooled = mm(values_ref[rows, cell : cell + KEYS_AT_ONCE], raw[:, lanes])
+        share = jnp.exp2(raw).astype(bf16)
+        sums = [
+            total + pool(cell, rows, share[:, lanes]) for total, (rows, lanes) in zip(sums, tiles)
+        ]
+    inside = []
+    for total, (rows, lanes) in zip(sums, tiles):
+        whole = total[-head_width : -head_width + 1]
+        inside.append((whole >= 1.0 / IN_RANGE) & (whole <= IN_RANGE))
+        pooled_ref[rows, lanes] = total[:-head_width] / whole
+    inside = jnp.min(jnp.concatenate(inside, axis=1).astype(f32))
+
+    @pl.when(inside < 0.5)
+    def _():
+        sums = [0.0] * len(tiles)
+        for cell in range(0, pixels, KEYS_AT_ONCE):
+            raw = raw_scores(cell)
+            top = fold_rows(raw, jnp.maximum)
             if cell > 0:
-                pooled = pooled + fade[:, lanes] * pooled_ref[rows, lanes]
-            if cell + KEYS_AT_ONCE == pixels:
-                pooled = pooled / total[:, lanes]
-            pooled_ref[rows, lanes] = pooled
-        old_top, old_total = top, total
+                top = jnp.maximum(top, old_top)
+                fade = jnp.exp2(old_top - top)
+                sums = [total * fade[:, lanes] for total, (rows, lanes) in zip(sums, tiles)]
+            old_top = top
+            share = jnp.exp2(raw - top).astype(bf16)
+            sums = [
+                total + pool(cell, rows, share[:, lanes])
+                for total, (rows, lanes) in zip(sums, tiles)
+            ]
+        for total, (rows, lanes) in zip(sums, tiles):
+            pooled_ref[rows, lanes] = total[:-head_width] / total[-head_width : -head_width + 1]
+
     joined = jnp.concatenate(
         [
             pooled_ref[h * head_width : (h + 1) * head_width, h * tokens : (h + 1) * tokens]
@@ -366,7 +389,10 @@
     scale = 1.0 / (SEAM + 1) ** 2
     to_left = scale * wide_mm(lines, jnp.maximum(left, 0).astype(f32).astype(bf16))
     to_right = scale * wide_mm(lines, jnp.maximum(right, 0).astype(f32).astype(bf16))
-    even = lax.rem(lax.axis_index("col"), 2) == 0
+    column = lax.axis_index("col")
+    to_left = jnp.where(column > 0, to_left, 0.0)
+    to_right = jnp.where(column < lax.axis_size("col") - 1, to_right, 0.0)
+    even = lax.rem(column, 2) == 0
     even_ref[...] = jnp.where(even, to_right, to_left)
     odd_ref[...] = jnp.where(even, to_left, to_right)
 
@@ -495,12 +521,21 @@
         name="decode",
     )(*arrays)
     count = lax.axis_size("col")
-    swaps = [
-        [pair for i in range(first, count - 1, 2) for pair in ((i, i + 1), (i + 1, i))]
-        for first in (0, 1)
-    ]
-    odd = lax.ppermute(odd, "col", swaps[1])
-    even = lax.ppermute(even, "col", swaps[0])
+    rows = lax.axis_size("row")
+    swaps = []
+    for first in (0, 1):
+        pairs = []
+        for row in range(rows):
+            for column in range(count):
+                other = column + 1 if column % 2 == first else column - 1
+                if 0 <= other < count:
+                    partner = row * count + other
+                else:
+                    partner = min(row ^ 1, rows - 1) * count + column
+                pairs.append((row * count + column, partner))
+        swaps.append(pairs)
+    odd = lax.ppermute(odd, ("row", "col"), swaps[1])
+    even = lax.ppermute(even, ("row", "col"), swaps[0])
     logits, blended = pl.pallas_call(
         image_kernel,
         out_shape=(shape((slots, pixels), bf16), shape((side, side), f32)),

time: 22 us -> 19.4 us (0.88)
  the two profiles are of different devices: /device:TPU:14 before, /device:TPU:0 now
where the time goes in v5:
time: 19.4 us; the launch traced here: 19.1 us
  Pallas kernels  14.7 us (76%)
  starting transfers between devices  3.12 us (16%)
  between operations  0.67 us (3%)
  other arithmetic  0.62 us (3%)
    pallas_call x1, Pallas kernels, shards(): pl.pallas_call(decode_kernel, out_shape=(shape((pixels, width), bf16), sh...  9.37 us
    pallas_call x1, Pallas kernels, shards(): pl.pallas_call(image_kernel, out_shape=(shape((slots, pixels), bf16), sha...  5.36 us
    ppermute x1, starting transfers between devices, shards(): even = lax.ppermute(even, ('row', 'col'), swaps[0])  3.12 us
    add x1, other arithmetic, shards(): return (logits.reshape(1, 1, slots, pixels), blended + even + odd)  0.62 us
  transfers between devices with their start and end apart: 2, of which 0 were waited for; matrix products, arithmetic and copies ran while one was open for 0% of the time, Pallas kernels for 28%

profile of v5, /device:TPU:0, one launch (start us, length us, event | category | flops | bytes accessed | tf_op | source)
XLA Modules:
  0.0 19.1 jit_solution(5539734653293524037)
XLA Ops:
  0.6 9.4 %decode.1 = (bf16[4096,256]{1,0:T(8,128)(2,1)S(1)}, bf16[4096,256]{1,0:T(8,128)(2,1)S(1)}, bf16[384,256]{1,0:T(8,128)(2,1)S(1)}, bf16[496,256]{1,0:T(8,128)(2,1)...) custom-call(s32[1,8]{1,0:T(1,128)} %counts_ref.1, ...), custom_call_target="tpu_custom_call" | custom-call | tf_op jit(solution)/shard_map/decode/pallas_call | solution.py:497
  10.0 3.1 %collective-permute-start = (f32[64,64]{1,0:T(8,128)S(1)}, f32[64,64]{1,0:T(8,128)S(1)}, u32[]{:S(2)}, u32[]{:S(2)}) collective-permute-start(f32[64,64]{1,0:T(8,128)S(1)} %get-tuple-element.20), channel_id=1, source_target_pairs={{0,1},{1,0},{2,3},{3,2},{4,5},{5,4},{6,7},{7,6},{8,9},{9,8},{10,11... | collective-permute-start | bytes 49160 | tf_op jit(solution)/shard_map/ppermute | solution.py:538
  13.1 0.0 collective-permute-start.1
  13.1 5.4 %image.1 = (bf16[48,4096]{1,0:T(8,128)(2,1)}, f32[64,64]{1,0:T(8,128)S(1)}) custom-call(s32[1,8]{1,0:T(1,128)} %counts_ref.1, bf16[4096,256]{1,0:T(8,128)(2,1)S(1)} %get-tuple-element.12.cells_ref, bf16[4096,256]{1,0:T(8,128)(2,1)S(1)} %get-tuple-element.13.keys_ref, bf16[384,256]{1,0:T(8,128)(2,1)S(1)} %get-tuple-element.14.gaps_ref, ...), custom_call_target="tpu_custom_call" | custom-call | tf_op jit(solution)/shard_map/image/pallas_call | solution.py:539
  18.5 0.0 collective-permute-done
  18.5 0.0 collective-permute-done.1
  18.5 0.6 %add_add_fusion = f32[64,64]{1,0:T(8,128)} fusion(f32[64,64]{1,0:T(8,128)S(1)} %collective-permute-done.1, f32[64,64]{1,0:T(8,128)S(1)} %get-tuple-element.19, f32[64,64]{1,0:T(8,128)S(1)} %collective-permute-done), kind=kLoop, calls=%fused_computation | loop fusion | flops 8192 | bytes 65536 | tf_op jit(solution)/shard_map/add | solution.py:552
Async XLA Ops:
  10.0 8.5 %collective-permute-start = (f32[64,64]{1,0:T(8,128)S(1)}, f32[64,64]{1,0:T(8,128)S(1)}, u32[]{:S(2)}, u32[]{:S(2)}) collective-permute-start(f32[64,64]{1,0:T(8,128)S(1)} %get-tuple-element.20), channel_id=1, source_target_pairs={{0,1},{1,0},{2,3},{3,2},{4,5},{5,4},{6,7},{7,6},{8,9},{9,8},{10,11... | collective-permute-start | bytes 49160 | tf_op jit(solution)/shard_map/ppermute | solution.py:538
  13.1 5.4 %collective-permute-start.1 = (f32[64,64]{1,0:T(8,128)S(1)}, f32[64,64]{1,0:T(8,128)S(1)}, u32[]{:S(2)}, u32[]{:S(2)}) collective-permute-start(f32[64,64]{1,0:T(8,128)S(1)} %get-tuple-element.21), channel_id=1, source_target_pairs={{0,4},{1,2},{2,1},{3,7},{4,0},{5,6},{6,5},{7,3},{8,12},{9,10},{10,... | collective-permute-start | bytes 49160 | tf_op jit(solution)/shard_map/ppermute | solution.py:537

commit v6 on v5

--- a/solution.py
+++ b/solution.py
@@ -107,17 +107,21 @@
     return jnp.where((column >= first) & (column < first + group), 1.0, 0.0).astype(bf16)
 
 
-def cell_weights(gaps, keys):
-    return jnp.tanh(mm_t(gaps, keys)).astype(bf16)
-
-
-def cell_logits(weights, cells, on_cells, on_weights, consts, live):
+def cell_weights(gaps, keys, on_cells, cells):
+    slots = gaps.shape[0] // HEADS
+    flat = mm_t(on_cells, cells)
+    weights = jnp.tanh(mm_t(gaps, keys)).astype(bf16)
+    return flat[:-slots].astype(bf16), weights, flat[-slots:]
+
+
+def cell_logits(found, cells, on_weights, consts, live):
+    folds, weights, products = found
     count, width = cells.shape
     slots = consts.shape[0]
     block = HEADS * SLOT_GROUP
     tall = block + 2 * SLOT_GROUP
-    flat = mm_t(on_cells, cells)
     wide = cells.astype(f32)
+    wide = wide - jnp.mean(wide, axis=1, keepdims=True)
     norms = jnp.sum(wide * wide, axis=1, keepdims=True)
     lanes = 128
     same = lax.broadcasted_iota(jnp.int32, (lanes, lanes), 0) == lax.broadcasted_iota(
@@ -130,20 +134,19 @@
         ],
         axis=1,
     )
-    total = flat[slots // SLOT_GROUP * tall :][:SLOT_GROUP]
-    norms = norms - total * total * (1.0 / width)
     logits, covers = [], []
     for at in range(0, slots, SLOT_GROUP):
         group = at // SLOT_GROUP
         mine = weights[group * block : (group + 1) * block]
-        both = flat[group * tall : (group + 1) * tall] + mm(
-            on_weights[group * tall : (group + 1) * tall], mine
+        both = mm(
+            on_weights[group * tall : (group + 1) * tall], jnp.concatenate([folds, mine], axis=0)
         )
         square = norms + both[block : block + SLOT_GROUP] + consts[at : at + SLOT_GROUP, 0:1]
         for h in range(HEADS):
             part = slice(h * SLOT_GROUP, (h + 1) * SLOT_GROUP)
             square = square + mine[part].astype(f32) * both[part]
-        dots = both[block + SLOT_GROUP :] + consts[at : at + SLOT_GROUP, 1:2]
+        dots = both[block + SLOT_GROUP :] + products[at : at + SLOT_GROUP]
+        dots = dots + consts[at : at + SLOT_GROUP, 1:2]
         kept = at + lax.broadcasted_iota(jnp.int32, (SLOT_GROUP, count), 0) < live
         found = dots * lax.rsqrt(jnp.maximum(square, 0.0) + width * norm_eps)
         found = jnp.where(kept, found, 0.0).astype(bf16)
@@ -337,6 +340,9 @@
     gaps = gaps.astype(bf16)
     middle = 0.5 * (back_v[:slots] + back_v[slots:])
     apart = by_group(0.5 * (back_v[:slots] - back_v[slots:]), inner)
+    twice = (2.0 * jnp.concatenate([apart, middle], axis=0)).astype(bf16)
+    out_wide = i2t_out_ref[...].astype(f32)
+    out_centred = (out_wide - jnp.mean(out_wide, axis=1, keepdims=True)).astype(bf16)
     moves = wide_mm(jnp.concatenate([apart, middle], axis=0), i2t_out_ref[...])
     moves = (moves - jnp.mean(moves, axis=1, keepdims=True)).astype(bf16)
     hyper = wide_mm(jnp.maximum(wide_mm(queries[:slots], hyper_ref[0]), 0.0), hyper_ref[1])
@@ -355,17 +361,23 @@
     tall = block + 2 * SLOT_GROUP
     row_slot = lax.rem(lax.broadcasted_iota(jnp.int32, (tall, block), 0), SLOT_GROUP)
     column_slot = lax.rem(lax.broadcasted_iota(jnp.int32, (tall, block), 1), SLOT_GROUP)
-    on_cells, on_weights = [], []
+    on_weights = []
     for at in range(0, slots, SLOT_GROUP):
         mine = apart[at * HEADS : (at + SLOT_GROUP) * HEADS]
-        mine_twice = (2.0 * mine.astype(f32)).astype(bf16)
         centre_twice = (2.0 * middle_wide[at : at + SLOT_GROUP]).astype(bf16)
         mask = hyper[at : at + SLOT_GROUP]
-        on_cells += [mine_twice, centre_twice, mask]
         crossed = mm_t(jnp.concatenate([mine, centre_twice, mask], axis=0), mine)
-        on_weights.append(jnp.where(row_slot == column_slot, crossed, 0.0).astype(bf16))
-    on_cells.append(jnp.ones((SLOT_GROUP, width), bf16))
-    on_cells = jnp.concatenate(on_cells, axis=0)
+        crossed = jnp.where(row_slot == column_slot, crossed, 0.0).astype(bf16)
+        folded = jnp.concatenate(
+            [
+                twice[at * HEADS : (at + SLOT_GROUP) * HEADS],
+                twice[HEADS * slots + at : HEADS * slots + at + SLOT_GROUP],
+                jnp.zeros((SLOT_GROUP, inner), bf16),
+            ],
+            axis=0,
+        )
+        on_weights.append(jnp.concatenate([folded, crossed], axis=1))
+    on_cells = jnp.concatenate([out_centred, hyper], axis=0)
     on_weights = jnp.concatenate(on_weights, axis=0)
     gaps_ref[...] = gaps
     on_cells_ref[...] = on_cells
@@ -373,10 +385,9 @@
     consts_ref[...] = consts
 
     live = counts_ref[0, lax.axis_index("row")]
-    weights = cell_weights(gaps, seam_keys_ref[...].astype(bf16))
-    _, covers = cell_logits(
-        weights, seam_cells_ref[...].astype(bf16), on_cells, on_weights, consts, live
-    )
+    seam_cells = seam_cells_ref[...].astype(bf16)
+    found = cell_weights(gaps, seam_keys_ref[...].astype(bf16), on_cells, seam_cells)
+    _, covers = cell_logits(found, seam_cells, on_weights, consts, live)
     count = 2 * SEAM * side
     line = lax.broadcasted_iota(jnp.int32, (side, count), 0)
     column = lax.broadcasted_iota(jnp.int32, (side, count), 1)
@@ -417,13 +428,17 @@
     gaps, on_cells, on_weights = gaps_ref[...], on_cells_ref[...], on_weights_ref[...]
     consts = consts_ref[...]
     places = [slice(at, at + CELLS_AT_ONCE) for at in range(0, pixels, CELLS_AT_ONCE)]
-    weights = cell_weights(gaps, keys_ref[places[0], :])
     copies = []
+
+    def begin(place):
+        return cell_weights(gaps, keys_ref[place, :], on_cells, cells_ref[place, :])
+
+    ahead = begin(places[0])
     for step, place in enumerate(places):
-        now = weights
+        found = ahead
         if step + 1 < len(places):
-            weights = cell_weights(gaps, keys_ref[places[step + 1], :])
-        logits, covers = cell_logits(now, cells_ref[place, :], on_cells, on_weights, consts, live)
+            ahead = begin(places[step + 1])
+        logits, covers = cell_logits(found, cells_ref[place, :], on_weights, consts, live)
         found_ref[:, place] = logits
         copies.append(
             pltpu.make_async_copy(found_ref.at[:, place], logits_ref.at[:, place], sems.at[step])
@@ -500,8 +515,8 @@
             shape((pixels, width), bf16),
             shape((pixels, width), bf16),
             shape((HEADS * slots, width), bf16),
-            shape((groups * tall + SLOT_GROUP, width), bf16),
-            shape((groups * tall, HEADS * SLOT_GROUP), bf16),
+            shape((inner + slots, width), bf16),
+            shape((groups * tall, inner + HEADS * SLOT_GROUP), bf16),
             shape((slots, 2), f32),
             shape((side, side), f32),
             shape((side, side), f32),

time: 19.4 us -> 19.3 us (level)
  transfers between devices with their start and end apart: 2 -> 2, of which waited for: 0 -> 0; matrix products, arithmetic and copies ran while one was open for 0% -> 0% of each run, Pallas kernels for 28% -> 27%
where the time goes in v6:
time: 19.3 us; the launch traced here: 19.1 us
  Pallas kernels  14.6 us (76%)
  starting transfers between devices  3.12 us (16%)
  between operations  0.67 us (3%)
  other arithmetic  0.62 us (3%)
    pallas_call x1, Pallas kernels, shards(): pl.pallas_call(decode_kernel, out_shape=(shape((pixels, width), bf16), sh...  9.43 us
    pallas_call x1, Pallas kernels, shards(): pl.pallas_call(image_kernel, out_shape=(shape((slots, pixels), bf16), sha...  5.21 us
    ppermute x1, starting transfers between devices, shards(): even = lax.ppermute(even, ('row', 'col'), swaps[0])  3.12 us
    add x1, other arithmetic, shards(): return (logits.reshape(1, 1, slots, pixels), blended + even + odd)  0.62 us
  transfers between devices with their start and end apart: 2, of which 0 were waited for; matrix products, arithmetic and copies ran while one was open for 0% of the time, Pallas kernels for 27%

profile of v6, /device:TPU:0, one launch (start us, length us, event | category | flops | bytes accessed | tf_op | source)
XLA Modules:
  0.0 19.1 jit_solution(4097960353466379454)
XLA Ops:
  0.6 9.4 %decode.1 = (bf16[4096,256]{1,0:T(8,128)(2,1)S(1)}, bf16[4096,256]{1,0:T(8,128)(2,1)S(1)}, bf16[384,256]{1,0:T(8,128)(2,1)S(1)}, bf16[176,256]{1,0:T(8,128)(2,1)...) custom-call(s32[1,8]{1,0:T(1,128)} %counts_ref.1, ...), custom_call_target="tpu_custom_call" | custom-call | tf_op jit(solution)/shard_map/decode/pallas_call | solution.py:512
  10.1 3.1 %collective-permute-start = (f32[64,64]{1,0:T(8,128)S(1)}, f32[64,64]{1,0:T(8,128)S(1)}, u32[]{:S(2)}, u32[]{:S(2)}) collective-permute-start(f32[64,64]{1,0:T(8,128)S(1)} %get-tuple-element.20), channel_id=1, source_target_pairs={{0,1},{1,0},{2,3},{3,2},{4,5},{5,4},{6,7},{7,6},{8,9},{9,8},{10,11... | collective-permute-start | bytes 49160 | tf_op jit(solution)/shard_map/ppermute | solution.py:553
  13.2 0.0 collective-permute-start.1
  13.2 5.2 %image.1 = (bf16[48,4096]{1,0:T(8,128)(2,1)}, f32[64,64]{1,0:T(8,128)S(1)}) custom-call(s32[1,8]{1,0:T(1,128)} %counts_ref.1, bf16[4096,256]{1,0:T(8,128)(2,1)S(1)} %get-tuple-element.12.cells_ref, bf16[4096,256]{1,0:T(8,128)(2,1)S(1)} %get-tuple-element.13.keys_ref, bf16[384,256]{1,0:T(8,128)(2,1)S(1)} %get-tuple-element.14.gaps_ref, ...), custom_call_target="tpu_custom_call" | custom-call | tf_op jit(solution)/shard_map/image/pallas_call | solution.py:554
  18.4 0.0 collective-permute-done
  18.4 0.0 collective-permute-done.1
  18.4 0.6 %add_add_fusion = f32[64,64]{1,0:T(8,128)} fusion(f32[64,64]{1,0:T(8,128)S(1)} %collective-permute-done.1, f32[64,64]{1,0:T(8,128)S(1)} %get-tuple-element.19, f32[64,64]{1,0:T(8,128)S(1)} %collective-permute-done), kind=kLoop, calls=%fused_computation | loop fusion | flops 8192 | bytes 65536 | tf_op jit(solution)/shard_map/add | solution.py:567
Async XLA Ops:
  10.1 8.3 %collective-permute-start = (f32[64,64]{1,0:T(8,128)S(1)}, f32[64,64]{1,0:T(8,128)S(1)}, u32[]{:S(2)}, u32[]{:S(2)}) collective-permute-start(f32[64,64]{1,0:T(8,128)S(1)} %get-tuple-element.20), channel_id=1, source_target_pairs={{0,1},{1,0},{2,3},{3,2},{4,5},{5,4},{6,7},{7,6},{8,9},{9,8},{10,11... | collective-permute-start | bytes 49160 | tf_op jit(solution)/shard_map/ppermute | solution.py:553
  13.2 5.2 %collective-permute-start.1 = (f32[64,64]{1,0:T(8,128)S(1)}, f32[64,64]{1,0:T(8,128)S(1)}, u32[]{:S(2)}, u32[]{:S(2)}) collective-permute-start(f32[64,64]{1,0:T(8,128)S(1)} %get-tuple-element.21), channel_id=1, source_target_pairs={{0,4},{1,2},{2,1},{3,7},{4,0},{5,6},{6,5},{7,3},{8,12},{9,10},{10,... | collective-permute-start | bytes 49160 | tf_op jit(solution)/shard_map/ppermute | solution.py:552

commit v7 on v6

--- a/solution.py
+++ b/solution.py
@@ -336,14 +336,14 @@
     back_k = wide_mm(queries + start, i2t_qkv_ref[:, inner : 2 * inner])
     back_v = wide_mm(queries, i2t_qkv_ref[:, 2 * inner :])
     gaps = by_group(back_k[:slots] - back_k[slots:], inner)
-    gaps = wide_mm(gaps, i2t_qkv_ref[:, :inner], mm_t) * (0.5 * head_scale)
+    gaps = mm_t(gaps.astype(bf16), i2t_qkv_ref[:, :inner]) * (0.5 * head_scale)
     gaps = gaps.astype(bf16)
     middle = 0.5 * (back_v[:slots] + back_v[slots:])
     apart = by_group(0.5 * (back_v[:slots] - back_v[slots:]), inner)
     twice = (2.0 * jnp.concatenate([apart, middle], axis=0)).astype(bf16)
     out_wide = i2t_out_ref[...].astype(f32)
     out_centred = (out_wide - jnp.mean(out_wide, axis=1, keepdims=True)).astype(bf16)
-    moves = wide_mm(jnp.concatenate([apart, middle], axis=0), i2t_out_ref[...])
+    moves = 0.5 * mm(twice, i2t_out_ref[...])
     moves = (moves - jnp.mean(moves, axis=1, keepdims=True)).astype(bf16)
     hyper = wide_mm(jnp.maximum(wide_mm(queries[:slots], hyper_ref[0]), 0.0), hyper_ref[1])
     hyper = hyper.astype(bf16).astype(f32) * gains_ref[3:4]

time: 19.3 us -> 19.2 us (level)
  transfers between devices with their start and end apart: 2 -> 2, of which waited for: 0 -> 0; matrix products, arithmetic and copies ran while one was open for 0% -> 0% of each run, Pallas kernels for 27% -> 28%
where the time goes in v7:
time: 19.2 us; the launch traced here: 18.9 us
  Pallas kernels  14.5 us (76%)
  starting transfers between devices  3.12 us (16%)
  between operations  0.67 us (3%)
  other arithmetic  0.62 us (3%)
    pallas_call x1, Pallas kernels, shards(): pl.pallas_call(decode_kernel, out_shape=(shape((pixels, width), bf16), sh...  9.31 us
    pallas_call x1, Pallas kernels, shards(): pl.pallas_call(image_kernel, out_shape=(shape((slots, pixels), bf16), sha...  5.22 us
    ppermute x1, starting transfers between devices, shards(): even = lax.ppermute(even, ('row', 'col'), swaps[0])  3.12 us
    add x1, other arithmetic, shards(): return (logits.reshape(1, 1, slots, pixels), blended + even + odd)  0.62 us
  transfers between devices with their start and end apart: 2, of which 0 were waited for; matrix products, arithmetic and copies ran while one was open for 0% of the time, Pallas kernels for 28%

profile of v7, /device:TPU:0, one launch (start us, length us, event | category | flops | bytes accessed | tf_op | source)
XLA Modules:
  0.0 18.9 jit_solution(17276534731622599867)
XLA Ops:
  0.6 9.3 %decode.1 = (bf16[4096,256]{1,0:T(8,128)(2,1)S(1)}, bf16[4096,256]{1,0:T(8,128)(2,1)S(1)}, bf16[384,256]{1,0:T(8,128)(2,1)S(1)}, bf16[176,256]{1,0:T(8,128)(2,1)...) custom-call(s32[1,8]{1,0:T(1,128)} %counts_ref.1, ...), custom_call_target="tpu_custom_call" | custom-call | tf_op jit(solution)/shard_map/decode/pallas_call | solution.py:512
  10.0 3.1 %collective-permute-start = (f32[64,64]{1,0:T(8,128)S(1)}, f32[64,64]{1,0:T(8,128)S(1)}, u32[]{:S(2)}, u32[]{:S(2)}) collective-permute-start(f32[64,64]{1,0:T(8,128)S(1)} %get-tuple-element.20), channel_id=1, source_target_pairs={{0,1},{1,0},{2,3},{3,2},{4,5},{5,4},{6,7},{7,6},{8,9},{9,8},{10,11... | collective-permute-start | bytes 49160 | tf_op jit(solution)/shard_map/ppermute | solution.py:553
  13.1 0.0 collective-permute-start.1
  13.1 5.2 %image.1 = (bf16[48,4096]{1,0:T(8,128)(2,1)}, f32[64,64]{1,0:T(8,128)S(1)}) custom-call(s32[1,8]{1,0:T(1,128)} %counts_ref.1, bf16[4096,256]{1,0:T(8,128)(2,1)S(1)} %get-tuple-element.12.cells_ref, bf16[4096,256]{1,0:T(8,128)(2,1)S(1)} %get-tuple-element.13.keys_ref, bf16[384,256]{1,0:T(8,128)(2,1)S(1)} %get-tuple-element.14.gaps_ref, ...), custom_call_target="tpu_custom_call" | custom-call | tf_op jit(solution)/shard_map/image/pallas_call | solution.py:554
  18.3 0.0 collective-permute-done
  18.3 0.0 collective-permute-done.1
  18.3 0.6 %add_add_fusion = f32[64,64]{1,0:T(8,128)} fusion(f32[64,64]{1,0:T(8,128)S(1)} %collective-permute-done.1, f32[64,64]{1,0:T(8,128)S(1)} %get-tuple-element.19, f32[64,64]{1,0:T(8,128)S(1)} %collective-permute-done), kind=kLoop, calls=%fused_computation | loop fusion | flops 8192 | bytes 65536 | tf_op jit(solution)/shard_map/add | solution.py:567
Async XLA Ops:
  10.0 8.3 %collective-permute-start = (f32[64,64]{1,0:T(8,128)S(1)}, f32[64,64]{1,0:T(8,128)S(1)}, u32[]{:S(2)}, u32[]{:S(2)}) collective-permute-start(f32[64,64]{1,0:T(8,128)S(1)} %get-tuple-element.20), channel_id=1, source_target_pairs={{0,1},{1,0},{2,3},{3,2},{4,5},{5,4},{6,7},{7,6},{8,9},{9,8},{10,11... | collective-permute-start | bytes 49160 | tf_op jit(solution)/shard_map/ppermute | solution.py:553
  13.1 5.2 %collective-permute-start.1 = (f32[64,64]{1,0:T(8,128)S(1)}, f32[64,64]{1,0:T(8,128)S(1)}, u32[]{:S(2)}, u32[]{:S(2)}) collective-permute-start(f32[64,64]{1,0:T(8,128)S(1)} %get-tuple-element.21), channel_id=1, source_target_pairs={{0,4},{1,2},{2,1},{3,7},{4,0},{5,6},{6,5},{7,3},{8,12},{9,10},{10,... | collective-permute-start | bytes 49160 | tf_op jit(solution)/shard_map/ppermute | solution.py:552
